TPU v7x, 256 devices: a whole 4x4x8 slice. The times are simulated.
256 devices in a mesh: section: 4 (over y), depth: 64 (over x, z, core).
Axes of the slice: x: 4, y: 4, z: 8, core: 2. Of those that a mesh axis runs over, the one named last changes fastest.
Arguments:
- alignment_input: bfloat16 [4, 2048, 32, 768], P('section', 'depth'), may hold values from -6 to 6
- target_slot: int32 [4, 2048], P('section', 'depth'), may hold values from -1 to 2047, as said below
- device_alignment: int32 [4, 64], P('section'), may hold values from 0 to 31, never falling along the last dimension, each value on 1 to 4 neighbouring positions
- layer_norm_gain: float32 [4, 768], P('section'), may hold values from 0.5 to 1.5
- layer_norm_bias: float32 [4, 768], P('section'), may hold values from -3 to 3
- query_key_value_weight: bfloat16 [4, 768, 2304], P('section'), may hold values from -1.25 to 1.25
- output_weight: bfloat16 [4, 768, 768], P('section'), may hold values from -0.21875 to 0.21875
Outputs:
- handed: bfloat16 [4, 2048, 32, 768], P('section', 'depth')
Inputs may be any that keep to these rules, and one draw needn't show every extreme that they name: `target_slot`: within a section no slot is named twice. The input slots of one device map to 16 devices, 2 consecutive slots each, at offsets along depth that are the same for every device of the section; empty slots carry -1. Every device receives at least 2 rows, in every draw some device sends 2 live rows to one device and some device receives 32 rows. `device_alignment`: an alignment's devices are consecutive, at most 4 of them, and every alignment holds at least one device.
All inputs are finite; a program needn't handle non-finite values.
Results may differ from a plain program's by a relative error of at most 0.0065.
Values may be sent and summed in bfloat16 or wider, within the bound.
No kernel may reach another device: no remote copies, remote signals or barrier semaphores. Data moves between devices by JAX's collectives and lax.ppermute only.
A program may use at most 128 MiB of HBM per device.

v0:
```python
import jax
import jax.numpy as jnp
from jax import lax
from jax.sharding import PartitionSpec as P

H = 12
DH = 64
SPAN = 4


EPSILON = 1e-05


def passed_along(value, axis, steps):
    count = lax.axis_size(axis)
    first, last = (max(0, -steps), min(count, count - steps))
    return lax.ppermute(value, axis, [(source, source + steps) for source in range(first, last)])


def passed_along_2(block, axis, distance):
    devices = range(lax.axis_size(axis))
    route = [((i - distance) % len(devices), i) for i in devices]
    return lax.ppermute(block, axis, route)


def normalize(incoming_rows, gain_row, offset):
    widened = incoming_rows.astype(jnp.float32)
    average = jnp.mean(widened, axis=-1, keepdims=True)
    centred = widened - average
    spread = jnp.mean(centred * centred, axis=-1, keepdims=True)
    return (centred * lax.rsqrt(spread + EPSILON) * gain_row + offset).astype(jnp.bfloat16)


def project(normed, weight_qkv):
    row_count, length, model_width = normed.shape
    packed = jnp.dot(
        normed.reshape(row_count * length, model_width),
        weight_qkv,
        preferred_element_type=jnp.float32,
    )
    return packed.astype(jnp.bfloat16).reshape(row_count, length, 3 * model_width)


def body(
    alignment_input,
    target_slot,
    device_alignment,
    layer_norm_gain,
    layer_norm_bias,
    query_key_value_weight,
    output_weight,
):
    incoming_rows = alignment_input[0]
    targets = target_slot[0]
    groups = device_alignment[0]
    row_count, length, model_width = incoming_rows.shape
    peer_count = lax.axis_size("depth")
    position = lax.axis_index("depth")
    capacity = max(2, (row_count + peer_count - 1) // peer_count)
    slot_count = peer_count * capacity
    sending = targets >= 0
    receiver = jnp.where(sending, targets // row_count, -1)
    placed = jnp.where(sending, targets % row_count, -1)
    by_peer = (receiver[:, None] == jnp.arange(peer_count)[None, :]).astype(jnp.int32)
    before = jnp.sum((jnp.cumsum(by_peer, axis=0) - 1) * by_peer, axis=1)
    send_index = jnp.where(sending, receiver * capacity + before, -1)
    picker = jnp.arange(slot_count)[:, None] == send_index[None, :]
    picker_bf = picker.astype(jnp.bfloat16)
    send_place = (jnp.sum(picker.astype(jnp.int32) * (placed + 1)[None, :], axis=1) - 1).reshape(
        peer_count, capacity
    )
    flattened = incoming_rows.reshape(row_count, -1)
    chosen = jnp.dot(picker_bf, flattened, preferred_element_type=jnp.float32).astype(jnp.bfloat16)
    got_rows = lax.all_to_all(
        chosen.reshape((peer_count, capacity) + incoming_rows.shape[1:]),
        "depth",
        split_axis=0,
        concat_axis=0,
        tiled=True,
    )
    got_place = lax.all_to_all(send_place, "depth", split_axis=0, concat_axis=0, tiled=True)
    putter = (jnp.arange(row_count)[:, None] == got_place.reshape(1, slot_count)).astype(
        jnp.bfloat16
    )
    flattened = got_rows.reshape(slot_count, -1)
    settled = jnp.dot(putter, flattened, preferred_element_type=jnp.float32).astype(jnp.bfloat16)
    balanced = settled.reshape((row_count,) + got_rows.shape[2:])
    packed = project(
        normalize(balanced, layer_norm_gain[0], layer_norm_bias[0]), query_key_value_weight[0]
    )
    live_rows = jnp.sum(
        (jnp.arange(row_count)[:, None] == got_place.reshape(1, slot_count)).astype(jnp.float32),
        axis=1,
    )
    head_shape = (row_count, length, H, DH)
    queries = (
        packed[:, :, :model_width].reshape(head_shape)
        * live_rows.astype(jnp.bfloat16)[:, None, None, None]
    )
    keys_all = packed[:, :, model_width : 2 * model_width].reshape(head_shape)
    values_all = packed[:, :, 2 * model_width :].reshape(head_shape)
    own_tied = jnp.einsum("mihd,mjhd->hij", queries, keys_all, preferred_element_type=jnp.float32)
    depth_own = jnp.sum(live_rows)
    own_group = groups[position]
    tied_sum = own_tied
    depth_total = depth_own
    for distance in range(1, min(SPAN, peer_count)):
        low_tied, low_depth = (
            passed_along(own_tied.astype(jnp.bfloat16), "depth", distance).astype(own_tied.dtype),
            passed_along(depth_own.astype(jnp.bfloat16), "depth", distance).astype(depth_own.dtype),
        )
        high_tied, high_depth = (
            passed_along(own_tied.astype(jnp.bfloat16), "depth", -distance).astype(own_tied.dtype),
            passed_along(depth_own.astype(jnp.bfloat16), "depth", -distance).astype(
                depth_own.dtype
            ),
        )
        same_low = jnp.logical_and(
            position - distance >= 0, groups[jnp.maximum(position - distance, 0)] == own_group
        )
        same_high = jnp.logical_and(
            position + distance <= peer_count - 1,
            groups[jnp.minimum(position + distance, peer_count - 1)] == own_group,
        )
        tied_sum = (
            tied_sum + jnp.where(same_low, low_tied, 0.0) + jnp.where(same_high, high_tied, 0.0)
        )
        depth_total = (
            depth_total
            + jnp.where(same_low, low_depth, 0.0)
            + jnp.where(same_high, high_depth, 0.0)
        )
    factor = DH ** (-0.5) / jnp.sqrt(depth_total)
    attention = jax.nn.softmax(tied_sum * factor, axis=-1).astype(jnp.bfloat16)
    attended = jnp.einsum(
        "hij,mjhd->mihd", attention, values_all, preferred_element_type=jnp.float32
    ).astype(jnp.bfloat16)
    mixed_out = jnp.dot(
        attended.reshape(row_count * length, model_width),
        output_weight[0],
        preferred_element_type=jnp.float32,
    )
    mixed_out = mixed_out + balanced.reshape(row_count * length, model_width).astype(jnp.float32)
    layer_out = (
        mixed_out.reshape(row_count, length, model_width) * live_rows[:, None, None]
    ).astype(jnp.bfloat16)
    return passed_along_2(layer_out[None], "section", 1)


def solution(mesh):
    placed = (
        P("section", "depth", None, None),
        P("section", "depth"),
        P("section", None),
        P("section", None),
        P("section", None),
        P("section", None, None),
        P("section", None, None),
    )
    return jax.shard_map(
        body,
        mesh=mesh,
        in_specs=placed,
        out_specs=P("section", "depth", None, None),
        check_vma=False,
    )
```

profile of v0, /device:TPU:2, one launch (start us, length us, event | category | flops | bytes accessed | tf_op | source)
XLA Modules:
  0.0 348.6 jit_solution(6612761251690503803)
XLA Ops:
  5.2 12.2 %all-to-all-start = ((s32[64,1,2]{2,1,0:T(1,128)}), s32[64,1,2]{2,1,0:T(1,128)}, u32[]{:S(2)}, u32[]{:S(2)}) async-start(s32[64,1,2]{2,1,0:T(1,128)} %bitcast.78), calls=%async_computation | async-start | bytes 65536 | tf_op jit(solution)/shard_map/all_to_all | solution.py:81
  21.6 4.5 %copy.31 = bf16[16,8,32,768]{3,2,1,0:T(8,128)(2,1)} copy(bf16[16,8,32,768]{3,1,2,0:T(8,128)(2,1)S(1)} %bitcast.68) | data formatting | bytes 12582912
  26.1 10.8 %all-to-all-start.1 = ((bf16[64,2,32,768]{3,2,1,0:T(8,128)(2,1)}), bf16[64,2,32,768]{3,2,1,0:T(8,128)(2,1)}, u32[]{:S(2)}, u32[]{:S(2)}) async-start(bf16[64,2,32,768]{3,2,1,0:T(8,128)(2,1)} %bitcast.67), calls=%async_computation.1 | async-start | bytes 12582912 | tf_op jit(solution)/shard_map/all_to_all | solution.py:74
  46.7 129.5 %all-to-all-done.1 = bf16[64,2,32,768]{3,2,1,0:T(8,128)(2,1)} async-done(((bf16[64,2,32,768]{3,2,1,0:T(8,128)(2,1)}), bf16[64,2,32,768]{3,2,1,0:T(8,128)(2,1)}, u32[]{:S(2)}, u32[]{:S(2)}) %all-to-all-start.1) | async-done | bytes 6291488 | tf_op jit(solution)/shard_map/all_to_all | solution.py:74
  176.3 7.0 %copy.32 = bf16[16,8,32,768]{3,1,2,0:T(8,128)(2,1)S(1)} copy(bf16[16,8,32,768]{3,2,1,0:T(8,128)(2,1)} %bitcast.28) | data formatting | bytes 12582912
  197.5 2.8 convert_element_type.126
  200.2 5.9 %convolution_convert_fusion.2 = bf16[1024,2304]{1,0:T(8,128)(2,1)S(1)} fusion(bf16[1024,768]{1,0:T(8,128)(2,1)} %convert_element_type.126, bf16[1,768,2304]{2,1,0:T(8,128)(2,1)S(1)} %copy-done), kind=kOutput, calls=%fused_computation.4 | convolution fusion | flops 3626237952 | bytes 9830400 | tf_op jit(solution)/shard_map/dot_general | solution.py:36
  207.9 3.8 %reshape.155 = bf16[32,32,12,64]{3,2,1,0:T(8,128)(2,1)} reshape(bf16[32,32,768]{2,1,0:T(8,128)(2,1)S(1)} %get-tuple-element.7) | data formatting | bytes 3145728 | tf_op jit(solution)/shard_map/reshape | solution.py:97
  211.7 3.8 %reshape.156 = bf16[32,32,12,64]{3,2,1,0:T(8,128)(2,1)} reshape(bf16[32,32,768]{2,1,0:T(8,128)(2,1)S(1)} %get-tuple-element.8) | data formatting | bytes 3145728 | tf_op jit(solution)/shard_map/reshape | solution.py:100
  221.4 4.2 %collective-permute-start.5 = (bf16[12,32,32]{1,2,0:T(8,128)(2,1)}, bf16[12,32,32]{1,2,0:T(8,128)(2,1)S(1)}, u32[]{:S(2)}, u32[]{:S(2)}) collective-permute-start(bf16[12,32,32]{1,2,0:T(8,128)(2,1)} %get-tuple-element.19), channel_id=1, source_target_pairs={{3,0},{4,1},{5,2},{6,3},{7,4},{8,5},{9,6},{10,7},{11,8},{12,9},{13... | collective-permute-start | bytes 73736 | tf_op jit(solution)/shard_map/ppermute | solution.py:17
  226.4 3.4 collective-permute-start.11
  229.7 4.2 %collective-permute-start.10 = (bf16[]{:T(256)}, bf16[]{:T(256)}, u32[]{:S(2)}, u32[]{:S(2)}) collective-permute-start(bf16[]{:T(256)} %convert_element_type.137), channel_id=1, source_target_pairs={{0,3},{1,4},{2,5},{3,6},{4,7},{5,8},{6,9},{7,10},{8,11},{9,12},{10... | collective-permute-start | bytes 14 | tf_op jit(solution)/shard_map/ppermute | solution.py:17
  233.9 5.9 %collective-permute-start.9 = (bf16[]{:T(256)}, bf16[]{:T(256)}, u32[]{:S(2)}, u32[]{:S(2)}) collective-permute-start(bf16[]{:T(256)} %convert_element_type.137), channel_id=1, source_target_pairs={{2,0},{3,1},{4,2},{5,3},{6,4},{7,5},{8,6},{9,7},{10,8},{11,9},{12,... | collective-permute-start | bytes 14 | tf_op jit(solution)/shard_map/ppermute | solution.py:17
  239.8 3.2 collective-permute-start.8
  243.0 7.3 %collective-permute-start.7 = (bf16[]{:T(256)}, bf16[]{:T(256)}, u32[]{:S(2)}, u32[]{:S(2)}) collective-permute-start(bf16[]{:T(256)} %convert_element_type.137), channel_id=1, source_target_pairs={{1,0},{2,1},{3,2},{4,3},{5,4},{6,5},{7,6},{8,7},{9,8},{10,9},{11,1... | collective-permute-start | bytes 14 | tf_op jit(solution)/shard_map/ppermute | solution.py:17
  250.2 2.7 collective-permute-start.6
  254.9 3.8 %collective-permute-start.3 = (bf16[12,32,32]{1,2,0:T(8,128)(2,1)}, bf16[12,32,32]{1,2,0:T(8,128)(2,1)}, u32[]{:S(2)}, u32[]{:S(2)}) collective-permute-start(bf16[12,32,32]{1,2,0:T(8,128)(2,1)} %get-tuple-element.19), channel_id=1, source_target_pairs={{2,0},{3,1},{4,2},{5,3},{6,4},{7,5},{8,6},{9,7},{10,8},{11,9},{12,... | collective-permute-start | bytes 73736 | tf_op jit(solution)/shard_map/ppermute | solution.py:17
  260.8 7.2 %collective-permute-start.1 = (bf16[12,32,32]{1,2,0:T(8,128)(2,1)}, bf16[12,32,32]{1,2,0:T(8,128)(2,1)}, u32[]{:S(2)}, u32[]{:S(2)}) collective-permute-start(bf16[12,32,32]{1,2,0:T(8,128)(2,1)} %get-tuple-element.19), channel_id=1, source_target_pairs={{1,0},{2,1},{3,2},{4,3},{5,4},{6,5},{7,6},{8,7},{9,8},{10,9},{11,1... | collective-permute-start | bytes 73736 | tf_op jit(solution)/shard_map/ppermute | solution.py:17
  284.7 5.9 %reshape.154 = bf16[32,32,12,64]{3,2,1,0:T(8,128)(2,1)} reshape(bf16[32,32,768]{2,1,0:T(8,128)(2,1)} %get-tuple-element.9) | data formatting | bytes 3145728 | tf_op jit(solution)/shard_map/reshape | solution.py:101
  292.5 4.0 %convert_bitcast_fusion = bf16[32,32,12,64]{3,1,0,2:T(8,128)(2,1)S(1)} fusion(bf16[32,32,12,64]{3,2,1,0:T(8,128)(2,1)} %reshape.154, f32[12,32]{1,0:T(8,128)S(1)} %fusion.28, f32[12,32,32]{1,2,0:T(8,128)S(1)} %add_multiply_fusion), kind=kOutput, calls=%fused_computation.12 | convolution fusion | flops 51155360 | bytes 3196416 | tf_op jit(solution)/shard_map/hij,mjhd->mihd/dot_general | solution.py:135
  296.5 5.2 %copy.25 = bf16[32,32,12,64]{3,2,1,0:T(8,128)(2,1)} copy(bf16[32,32,12,64]{3,1,0,2:T(8,128)(2,1)S(1)} %convert_bitcast_fusion) | data formatting | bytes 3145728 | tf_op jit(solution)/shard_map/convert_element_type | solution.py:137
  301.7 6.2 %reshape.157 = bf16[1024,768]{1,0:T(8,128)(2,1)} reshape(bf16[32,32,12,64]{3,2,1,0:T(8,128)(2,1)} %copy.25) | data formatting | bytes 3145728 | tf_op jit(solution)/shard_map/reshape | solution.py:139
  307.9 3.1 convolution_add_fusion
  313.2 34.3 %collective-permute-done.12 = bf16[1,32,32,768]{3,2,1,0:T(8,128)(2,1)S(1)} collective-permute-done((bf16[1,32,32,768]{3,2,1,0:T(8,128)(2,1)S(1)}, bf16[1,32,32,768]{3,2,1,0:T(8,128)(2,1)S(1)}, u32[]{:S(2)}, u32[]{:S(2)}) %collective-permute-start.12) | collective-permute-done | bytes 1572896 | tf_op jit(solution)/shard_map/ppermute | solution.py:23
  (96 shorter events, 54.7 us)
Async XLA Ops:
  0.0 200.2 %copy-start = (bf16[1,768,2304]{2,1,0:T(8,128)(2,1)S(1)}, bf16[1,768,2304]{2,1,0:T(8,128)(2,1)}, u32[]{:S(2)}) copy-start(bf16[1,768,2304]{2,1,0:T(8,128)(2,1)} %param.12) | copy-start | bytes 10616836
  5.2 20.9 %all-to-all-start = ((s32[64,1,2]{2,1,0:T(1,128)}), s32[64,1,2]{2,1,0:T(1,128)}, u32[]{:S(2)}, u32[]{:S(2)}) async-start(s32[64,1,2]{2,1,0:T(1,128)} %bitcast.78), calls=%async_computation | async-start | bytes 65536 | tf_op jit(solution)/shard_map/all_to_all | solution.py:81
  26.1 10.8 %copy-start.13 = (f32[1,768]{1,0:T(1,128)S(1)}, f32[1,768]{1,0:T(1,128)}, u32[]{:S(2)}) copy-start(f32[1,768]{1,0:T(1,128)} %param.10) | copy-start | bytes 9220
  26.1 10.8 %copy-start.14 = (f32[1,768]{1,0:T(1,128)S(1)}, f32[1,768]{1,0:T(1,128)}, u32[]{:S(2)}) copy-start(f32[1,768]{1,0:T(1,128)} %param.11) | copy-start | bytes 9220
  26.1 150.1 %all-to-all-start.1 = ((bf16[64,2,32,768]{3,2,1,0:T(8,128)(2,1)}), bf16[64,2,32,768]{3,2,1,0:T(8,128)(2,1)}, u32[]{:S(2)}, u32[]{:S(2)}) async-start(bf16[64,2,32,768]{3,2,1,0:T(8,128)(2,1)} %bitcast.67), calls=%async_computation.1 | async-start | bytes 12582912 | tf_op jit(solution)/shard_map/all_to_all | solution.py:74
  219.0 51.0 %copy-start.12 = (s32[1,64]{1,0:T(1,128)S(1)}, s32[1,64]{1,0:T(1,128)}, u32[]{:S(2)}) copy-start(s32[1,64]{1,0:T(1,128)} %param.9) | copy-start | bytes 772
  219.0 63.4 %copy-start.4 = (f32[32,24576]{1,0:T(8,128)S(1)}, f32[32,24576]{1,0:T(8,128)}, u32[]{:S(2)}) copy-start(f32[32,24576]{1,0:T(8,128)} %copy-done.2) | copy-start | bytes 9437188
  221.4 46.6 %collective-permute-start.5 = (bf16[12,32,32]{1,2,0:T(8,128)(2,1)}, bf16[12,32,32]{1,2,0:T(8,128)(2,1)S(1)}, u32[]{:S(2)}, u32[]{:S(2)}) collective-permute-start(bf16[12,32,32]{1,2,0:T(8,128)(2,1)} %get-tuple-element.19), channel_id=1, source_target_pairs={{3,0},{4,1},{5,2},{6,3},{7,4},{8,5},{9,6},{10,7},{11,8},{12,9},{13... | collective-permute-start | bytes 73736 | tf_op jit(solution)/shard_map/ppermute | solution.py:17
  226.4 16.6 %collective-permute-start.11 = (bf16[]{:T(256)}, bf16[]{:T(256)}, u32[]{:S(2)}, u32[]{:S(2)}) collective-permute-start(bf16[]{:T(256)} %convert_element_type.137), channel_id=1, source_target_pairs={{3,0},{4,1},{5,2},{6,3},{7,4},{8,5},{9,6},{10,7},{11,8},{12,9},{13... | collective-permute-start | bytes 14 | tf_op jit(solution)/shard_map/ppermute | solution.py:17
  229.7 20.5 %collective-permute-start.10 = (bf16[]{:T(256)}, bf16[]{:T(256)}, u32[]{:S(2)}, u32[]{:S(2)}) collective-permute-start(bf16[]{:T(256)} %convert_element_type.137), channel_id=1, source_target_pairs={{0,3},{1,4},{2,5},{3,6},{4,7},{5,8},{6,9},{7,10},{8,11},{9,12},{10... | collective-permute-start | bytes 14 | tf_op jit(solution)/shard_map/ppermute | solution.py:17
  233.9 19.1 %collective-permute-start.9 = (bf16[]{:T(256)}, bf16[]{:T(256)}, u32[]{:S(2)}, u32[]{:S(2)}) collective-permute-start(bf16[]{:T(256)} %convert_element_type.137), channel_id=1, source_target_pairs={{2,0},{3,1},{4,2},{5,3},{6,4},{7,5},{8,6},{9,7},{10,8},{11,9},{12,... | collective-permute-start | bytes 14 | tf_op jit(solution)/shard_map/ppermute | solution.py:17
  239.8 15.1 %collective-permute-start.8 = (bf16[]{:T(256)}, bf16[]{:T(256)}, u32[]{:S(2)}, u32[]{:S(2)}) collective-permute-start(bf16[]{:T(256)} %convert_element_type.137), channel_id=1, source_target_pairs={{0,2},{1,3},{2,4},{3,5},{4,6},{5,7},{6,8},{7,9},{8,10},{9,11},{10,... | collective-permute-start | bytes 14 | tf_op jit(solution)/shard_map/ppermute | solution.py:17
  243.0 15.8 %collective-permute-start.7 = (bf16[]{:T(256)}, bf16[]{:T(256)}, u32[]{:S(2)}, u32[]{:S(2)}) collective-permute-start(bf16[]{:T(256)} %convert_element_type.137), channel_id=1, source_target_pairs={{1,0},{2,1},{3,2},{4,3},{5,4},{6,5},{7,6},{8,7},{9,8},{10,9},{11,1... | collective-permute-start | bytes 14 | tf_op jit(solution)/shard_map/ppermute | solution.py:17
  250.2 10.5 %collective-permute-start.6 = (bf16[]{:T(256)}, bf16[]{:T(256)}, u32[]{:S(2)}, u32[]{:S(2)}) collective-permute-start(bf16[]{:T(256)} %convert_element_type.137), channel_id=1, source_target_pairs={{0,1},{1,2},{2,3},{3,4},{4,5},{5,6},{6,7},{7,8},{8,9},{9,10},{10,1... | collective-permute-start | bytes 14 | tf_op jit(solution)/shard_map/ppermute | solution.py:17
  253.0 37.6 %collective-permute-start.4 = (bf16[12,32,32]{1,2,0:T(8,128)(2,1)}, bf16[12,32,32]{1,2,0:T(8,128)(2,1)S(1)}, u32[]{:S(2)}, u32[]{:S(2)}) collective-permute-start(bf16[12,32,32]{1,2,0:T(8,128)(2,1)} %get-tuple-element.19), channel_id=1, source_target_pairs={{0,3},{1,4},{2,5},{3,6},{4,7},{5,8},{6,9},{7,10},{8,11},{9,12},{10... | collective-permute-start | bytes 73736 | tf_op jit(solution)/shard_map/ppermute | solution.py:17
  254.9 35.7 %collective-permute-start.3 = (bf16[12,32,32]{1,2,0:T(8,128)(2,1)}, bf16[12,32,32]{1,2,0:T(8,128)(2,1)}, u32[]{:S(2)}, u32[]{:S(2)}) collective-permute-start(bf16[12,32,32]{1,2,0:T(8,128)(2,1)} %get-tuple-element.19), channel_id=1, source_target_pairs={{2,0},{3,1},{4,2},{5,3},{6,4},{7,5},{8,6},{9,7},{10,8},{11,9},{12,... | collective-permute-start | bytes 73736 | tf_op jit(solution)/shard_map/ppermute | solution.py:17
  258.7 31.9 %collective-permute-start.2 = (bf16[12,32,32]{1,2,0:T(8,128)(2,1)}, bf16[12,32,32]{1,2,0:T(8,128)(2,1)}, u32[]{:S(2)}, u32[]{:S(2)}) collective-permute-start(bf16[12,32,32]{1,2,0:T(8,128)(2,1)} %get-tuple-element.19), channel_id=1, source_target_pairs={{0,2},{1,3},{2,4},{3,5},{4,6},{5,7},{6,8},{7,9},{8,10},{9,11},{10,... | collective-permute-start | bytes 73736 | tf_op jit(solution)/shard_map/ppermute | solution.py:17
  260.8 29.8 %collective-permute-start.1 = (bf16[12,32,32]{1,2,0:T(8,128)(2,1)}, bf16[12,32,32]{1,2,0:T(8,128)(2,1)}, u32[]{:S(2)}, u32[]{:S(2)}) collective-permute-start(bf16[12,32,32]{1,2,0:T(8,128)(2,1)} %get-tuple-element.19), channel_id=1, source_target_pairs={{1,0},{2,1},{3,2},{4,3},{5,4},{6,5},{7,6},{8,7},{9,8},{10,9},{11,1... | collective-permute-start | bytes 73736 | tf_op jit(solution)/shard_map/ppermute | solution.py:17
  268.0 16.7 %copy-start.9 = (bf16[12,32,32]{1,2,0:T(8,128)(2,1)}, bf16[12,32,32]{1,2,0:T(8,128)(2,1)S(1)}, u32[]{:S(2)}) copy-start(bf16[12,32,32]{1,2,0:T(8,128)(2,1)S(1)} %collective-permute-done.5) | copy-start | bytes 73732
  268.0 22.6 %collective-permute-start = (bf16[12,32,32]{1,2,0:T(8,128)(2,1)}, bf16[12,32,32]{1,2,0:T(8,128)(2,1)}, u32[]{:S(2)}, u32[]{:S(2)}) collective-permute-start(bf16[12,32,32]{1,2,0:T(8,128)(2,1)} %get-tuple-element.19), channel_id=1, source_target_pairs={{0,1},{1,2},{2,3},{3,4},{4,5},{5,6},{6,7},{7,8},{8,9},{9,10},{10,1... | collective-permute-start | bytes 73736 | tf_op jit(solution)/shard_map/ppermute | solution.py:17
  284.7 6.6 %copy-start.10 = (bf16[12,32,32]{1,2,0:T(8,128)(2,1)S(1)}, bf16[12,32,32]{1,2,0:T(8,128)(2,1)}, u32[]{:S(2)}) copy-start(bf16[12,32,32]{1,2,0:T(8,128)(2,1)} %copy-done.9) | copy-start | bytes 73732
  301.7 6.2 %copy-start.6 = (f32[1024,768]{1,0:T(8,128)S(1)}, f32[1024,768]{1,0:T(8,128)}, u32[]{:S(2)}) copy-start(f32[1024,768]{1,0:T(8,128)} %reshape.160) | copy-start | bytes 9437188
  311.1 37.5 %copy-start.1 = (bf16[1,768,2304]{2,1,0:T(8,128)(2,1)S(1)}, bf16[1,768,2304]{2,1,0:T(8,128)(2,1)}, u32[]{:S(2)}) copy-start(bf16[1,768,2304]{2,1,0:T(8,128)(2,1)} %param.12) | copy-start | bytes 10616836
  311.5 35.9 %collective-permute-start.12 = (bf16[1,32,32,768]{3,2,1,0:T(8,128)(2,1)S(1)}, bf16[1,32,32,768]{3,2,1,0:T(8,128)(2,1)S(1)}, u32[]{:S(2)}, u32[]{:S(2)}) collective-permute-start(bf16[1,32,32,768]{3,2,1,0:T(8,128)(2,1)S(1)} %multiply_convert_fusion), channel_id=1, source_target_pairs={{192,0},{0,64},{64,128},{128,192},{193,1},{1,65},{65,129},{129,193... | collective-permute-start | bytes 4718600 | tf_op jit(solution)/shard_map/ppermute | solution.py:23
  (10 other events, 20.5 us)
where the time goes:
time: 350 us; the launch traced here: 349 us
  waiting for transfers between devices  164 us (47%)
  starting transfers between devices  72.4 us (21%)
  local copies, waits for them, and re-layouts  63.3 us (18%)
  matrix products  18.2 us (5%)
  other arithmetic  17.9 us (5%)
  between operations  12.9 us (4%)
    all_to_all x1, waiting for transfers between devices, body(): lax.all_to_all(chosen.reshape((peer_count, capacity) + incoming_rows.shap...  130 us
    ppermute x12, starting transfers between devices, passed_along(): lax.ppermute(value, axis, [(source, source + steps) for source in range(f...  47.7 us
    ppermute x1, waiting for transfers between devices, passed_along_2(): return lax.ppermute(block, axis, route)  34.3 us
    unnamed x45, local copies, waits for them, and re-layouts  23.8 us
    all_to_all x1, starting transfers between devices, body(): lax.all_to_all(send_place, 'depth', split_axis=0, concat_axis=0, tiled=True)  12.2 us
    all_to_all x1, starting transfers between devices, body(): lax.all_to_all(chosen.reshape((peer_count, capacity) + incoming_rows.shap...  10.8 us
  transfers between devices with their start and end apart: 15, of which 2 were waited for; matrix products, arithmetic and copies ran while one was open for 8% of the time, Pallas kernels for 0%

commit v1 on v0

v1 whole, which is shorter than its diff:
```python
import functools

import jax
import jax.numpy as jnp
from jax import lax
from jax.experimental import pallas as pl
from jax.experimental.pallas import tpu as pltpu
from jax.sharding import PartitionSpec as P

H = 12
DH = 64
SPAN = 4
PAIRS = H // 2
EPSILON = 1e-05
CHUNK_ROWS = 8
INTERPRET = False


def spread_kernel(slot_ref, rows_ref, out_ref, sem):
    count = rows_ref.shape[0]

    def copy_of(i):
        return pltpu.make_async_copy(
            rows_ref.at[i], out_ref.at[jnp.maximum(slot_ref[i], 0)], sem.at[i]
        )

    for i in range(count):

        @pl.when(slot_ref[i] >= 0)
        def _():
            copy_of(i).start()

    for i in range(count):

        @pl.when(slot_ref[i] >= 0)
        def _():
            copy_of(i).wait()


def spread(rows, slots, slot_count):
    return pl.pallas_call(
        spread_kernel,
        out_shape=jax.ShapeDtypeStruct((slot_count,) + rows.shape[1:], rows.dtype),
        in_specs=[
            pl.BlockSpec(memory_space=pltpu.SMEM),
            pl.BlockSpec(memory_space=pl.ANY),
        ],
        out_specs=pl.BlockSpec(memory_space=pl.ANY),
        scratch_shapes=[pltpu.SemaphoreType.DMA((rows.shape[0],))],
        interpret=INTERPRET,
    )(slots, rows)


def lane_mask(shape):
    return lax.broadcasted_iota(jnp.int32, shape, len(shape) - 1) % 128 < DH


def front_kernel(
    source_ref,
    rows_ref,
    gain_ref,
    bias_ref,
    weight_ref,
    balanced_ref,
    values_ref,
    tied_ref,
    tied_low_ref,
    landed,
    acc,
    sem,
):
    row_count = source_ref.shape[0]
    length, width = rows_ref.shape[1:]
    copies = [
        pltpu.make_async_copy(
            rows_ref.at[jnp.maximum(source_ref[m], 0)], landed.at[m], sem.at[m]
        )
        for m in range(row_count)
    ]
    for copy in copies:
        copy.start()
    gain = gain_ref[...]
    bias = bias_ref[...]
    weight = weight_ref[...]
    first = lane_mask((length, 256))
    for start in range(0, row_count, CHUNK_ROWS):
        members = range(start, start + CHUNK_ROWS)
        pieces = []
        for m in members:
            copies[m].wait()
            pieces.append(
                jnp.where(source_ref[m] >= 0, landed[m], jnp.zeros_like(landed[m]))
            )
        block = jnp.concatenate(pieces, axis=0)
        tokens = pl.ds(start * length, CHUNK_ROWS * length)
        balanced_ref[tokens, :] = block
        widened = block.astype(jnp.float32)
        average = jnp.mean(widened, axis=-1, keepdims=True)
        centred = widened - average
        spread_of = jnp.mean(centred * centred, axis=-1, keepdims=True)
        normed = (centred * lax.rsqrt(spread_of + EPSILON) * gain + bias).astype(jnp.bfloat16)
        packed = jnp.dot(normed, weight, preferred_element_type=jnp.float32).astype(jnp.bfloat16)
        values_ref[tokens, :] = packed[:, 2 * width :]
        for pair in range(PAIRS):
            lanes = slice(pair * 128, pair * 128 + 128)
            key_lanes = slice(width + pair * 128, width + pair * 128 + 128)
            total = None
            for r in range(0, CHUNK_ROWS, 2):
                query_parts = []
                key_parts = []
                for k in (r, r + 1):
                    own = slice(k * length, (k + 1) * length)
                    query = packed[own, lanes]
                    query_parts.append(
                        jnp.where(source_ref[start + k] >= 0, query, jnp.zeros_like(query))
                    )
                    key_parts.append(packed[own, key_lanes])
                query = jnp.concatenate(query_parts, axis=1)
                key = jnp.concatenate(key_parts, axis=1)
                zero = jnp.zeros_like(query)
                both = jnp.concatenate(
                    [jnp.where(first, query, zero), jnp.where(first, zero, query)], axis=0
                )
                part = lax.dot_general(
                    both, key, (((1,), (1,)), ((), ())), preferred_element_type=jnp.float32
                )
                total = part if total is None else total + part
            own = pl.ds(pair * 2 * length, 2 * length)
            if start == 0:
                acc[own, :] = total
            else:
                acc[own, :] += total
    quarter = H * length // 4
    tied = jnp.concatenate(
        [acc[pl.ds(q * quarter, quarter), :] for q in range(4)], axis=1
    )
    tied_ref[...] = tied
    tied_low_ref[...] = tied.astype(jnp.bfloat16)


def front(source, rows, gain, bias, weight):
    row_count = source.shape[0]
    length, width = rows.shape[1:]
    tokens = row_count * length
    quarter = H * length // 4
    vmem = pl.BlockSpec(memory_space=pltpu.VMEM)
    return pl.pallas_call(
        front_kernel,
        out_shape=(
            jax.ShapeDtypeStruct((tokens, width), jnp.bfloat16),
            jax.ShapeDtypeStruct((tokens, width), jnp.bfloat16),
            jax.ShapeDtypeStruct((quarter, 4 * length), jnp.float32),
            jax.ShapeDtypeStruct((quarter, 4 * length), jnp.bfloat16),
        ),
        in_specs=[
            pl.BlockSpec(memory_space=pltpu.SMEM),
            pl.BlockSpec(memory_space=pl.ANY),
            vmem,
            vmem,
            vmem,
        ],
        out_specs=(vmem, vmem, vmem, vmem),
        scratch_shapes=[
            pltpu.VMEM((row_count, length, width), jnp.bfloat16),
            pltpu.VMEM((H * length, length), jnp.float32),
            pltpu.SemaphoreType.DMA((row_count,)),
        ],
        compiler_params=pltpu.CompilerParams(vmem_limit_bytes=40 << 20),
        interpret=INTERPRET,
    )(source, rows, gain, bias, weight)


def attention_of(tied, scale, length):
    quarter = tied.shape[0]
    logits = (
        jnp.concatenate([tied[:, q * length : (q + 1) * length] for q in range(4)], axis=0) * scale
    )
    top = jnp.max(logits, axis=-1, keepdims=True)
    raised = jnp.exp(logits - top)
    return (raised / jnp.sum(raised, axis=-1, keepdims=True)).astype(jnp.bfloat16)


def back_kernel(
    source_ref,
    flag_ref,
    balanced_ref,
    values_ref,
    tied_ref,
    n1_ref,
    n2_ref,
    n3_ref,
    n4_ref,
    n5_ref,
    n6_ref,
    weight_ref,
    out_ref,
):
    row_count = source_ref.shape[0]
    length = out_ref.shape[0] // row_count
    width = out_ref.shape[1]
    tied = tied_ref[...]
    for place, ref in enumerate((n1_ref, n2_ref, n3_ref, n4_ref, n5_ref, n6_ref)):
        tied = tied + jnp.where(flag_ref[place] > 0, ref[...].astype(jnp.float32), 0.0)
    attention = attention_of(tied, flag_ref[6], length)
    span = CHUNK_ROWS * length
    wide = jnp.concatenate([attention] * CHUNK_ROWS, axis=1)
    diagonal = (
        lax.broadcasted_iota(jnp.int32, (span, span), 0) // length
        == lax.broadcasted_iota(jnp.int32, (span, span), 1) // length
    )
    first = lane_mask((span, 128))
    mixers = []
    for h in range(H):
        tall = jnp.concatenate([wide[h * length : (h + 1) * length]] * CHUNK_ROWS, axis=0)
        mixers.append(jnp.where(diagonal, tall, jnp.zeros_like(tall)))
    weight = weight_ref[...]
    for start in range(0, row_count, CHUNK_ROWS):
        tokens = pl.ds(start * length, span)
        values = values_ref[tokens, :]
        parts = []
        for pair in range(PAIRS):
            lanes = values[:, pair * 128 : pair * 128 + 128]
            low = jnp.dot(mixers[2 * pair], lanes, preferred_element_type=jnp.float32)
            high = jnp.dot(mixers[2 * pair + 1], lanes, preferred_element_type=jnp.float32)
            parts.append(jnp.where(first, low, high).astype(jnp.bfloat16))
        attended = jnp.concatenate(parts, axis=1)
        mixed = jnp.dot(attended, weight, preferred_element_type=jnp.float32)
        mixed = (mixed + balanced_ref[tokens, :].astype(jnp.float32)).astype(jnp.bfloat16)
        for k in range(CHUNK_ROWS):
            own = mixed[k * length : (k + 1) * length]
            out_ref[pl.ds((start + k) * length, length), :] = jnp.where(
                source_ref[start + k] >= 0, own, jnp.zeros_like(own)
            )


def back(source, flags, balanced, values, tied, neighbours, weight):
    vmem = pl.BlockSpec(memory_space=pltpu.VMEM)
    smem = pl.BlockSpec(memory_space=pltpu.SMEM)
    return pl.pallas_call(
        back_kernel,
        out_shape=jax.ShapeDtypeStruct(balanced.shape, jnp.bfloat16),
        in_specs=[smem, smem] + [vmem] * 10,
        out_specs=vmem,
        compiler_params=pltpu.CompilerParams(vmem_limit_bytes=40 << 20),
        interpret=INTERPRET,
    )(source, flags, balanced, values, tied, *neighbours, weight)


def shifted(value, axis, steps, wrap):
    count = lax.axis_size(axis)
    if wrap:
        route = [(i, (i + steps) % count) for i in range(count)]
    else:
        route = [(i, i + steps) for i in range(count) if 0 <= i + steps < count]
    return lax.ppermute(value, axis, route)


def body(
    alignment_input,
    target_slot,
    device_alignment,
    layer_norm_gain,
    layer_norm_bias,
    query_key_value_weight,
    output_weight,
):
    incoming = alignment_input[0]
    targets = target_slot[0]
    groups = device_alignment[0]
    row_count, length, width = incoming.shape
    peers = lax.axis_size("depth")
    position = lax.axis_index("depth")
    capacity = max(2, (row_count + peers - 1) // peers)
    slots = jnp.where(
        targets >= 0,
        targets // row_count * capacity + jnp.arange(row_count) % capacity,
        -1,
    )
    outgoing = spread(incoming, slots, peers * capacity)
    got = lax.all_to_all(
        outgoing.reshape((peers, capacity, length, width)),
        "depth",
        split_axis=0,
        concat_axis=0,
        tiled=True,
    ).reshape(peers * capacity, length, width)
    everywhere = lax.all_to_all(
        jnp.broadcast_to(targets[None], (peers, row_count)),
        "depth",
        split_axis=0,
        concat_axis=0,
        tiled=True,
    )
    local = everywhere - position * row_count
    mine = jnp.logical_and(local >= 0, local < row_count)
    code = (
        lax.broadcasted_iota(jnp.int32, (peers, row_count), 0) * capacity
        + lax.broadcasted_iota(jnp.int32, (peers, row_count), 1) % capacity
    )
    wanted = jnp.where(mine, local, -1).reshape(1, -1)
    hit = jnp.arange(row_count)[:, None] == wanted
    source = jnp.max(jnp.where(hit, code.reshape(1, -1), -1), axis=1)
    own_group = groups[position]
    low = jnp.sum((groups < own_group).astype(jnp.int32))
    high = low + jnp.sum((groups == own_group).astype(jnp.int32))
    inside = jnp.logical_and(everywhere >= low * row_count, everywhere < high * row_count)
    depth_total = jnp.sum(inside.astype(jnp.float32))
    balanced, values, tied, tied_low = front(
        source, got, layer_norm_gain, layer_norm_bias, query_key_value_weight[0]
    )
    steps = [d for k in range(1, SPAN) for d in (k, -k)]
    neighbours = [shifted(tied_low, "depth", d, False) for d in steps]
    flags = [
        jnp.logical_and(position - d >= low, position - d < high).astype(jnp.float32)
        for d in steps
    ]
    flags = jnp.stack(flags + [DH ** (-0.5) / jnp.sqrt(depth_total)])
    layer_out = back(source, flags, balanced, values, tied, neighbours, output_weight[0])
    return shifted(layer_out.reshape(1, row_count, length, width), "section", 1, True)


def solution(mesh):
    placed = (
        P("section", "depth", None, None),
        P("section", "depth"),
        P("section", None),
        P("section", None),
        P("section", None),
        P("section", None, None),
        P("section", None, None),
    )
    return jax.shard_map(
        body,
        mesh=mesh,
        in_specs=placed,
        out_specs=P("section", "depth", None, None),
        check_vma=False,
    )
```

time: 350 us -> 303 us (0.87)
  Pallas kernels: 0 us -> 52.4 us
  local copies, waits for them, and re-layouts: 63.3 us -> 14.6 us
  starting transfers between devices: 72.4 us -> 50.5 us
  matrix products: 18.2 us -> 0 us
  other arithmetic: 17.9 us -> 6.85 us
  waiting for transfers between devices: 164 us -> 171 us
  between operations: 12.9 us -> 6.54 us
    pallas_call x0 -> x3, Pallas kernels: none -> 52.4 us  [the longest x1 39.3 us: spread(): pl.pallas_call(spread_kernel, out_shape=jax.ShapeDtypeStruct((slot_count,...]
    ppermute x13 -> x7, starting transfers between devices: 49.4 us -> 21.2 us  [shifted(): return lax.ppermute(value, axis, route)]
    reshape x4 -> x0, local copies, waits for them, and re-layouts: 19.8 us -> none  [the longest x1 6.23 us: body(): attended.reshape(row_count * length, model_width)]
    dot_general x6 -> x0, matrix products: 18.2 us -> none  [the longest x1 5.85 us: project(): jnp.dot(normed.reshape(row_count * length, model_width), weight_qkv, pref...]
    unnamed x45 -> x23, local copies, waits for them, and re-layouts: 23.8 us -> 8.95 us
    convert_element_type x3 -> x0, local copies, waits for them, and re-layouts: 10.1 us -> none  [the longest x1 5.17 us: body(): attended = jnp.einsum('hij,mjhd->mihd', attention, values_all, preferred_...]
    all_to_all x2, starting transfers between devices: 23 us -> 29.3 us  [the longest x1 17 us: body(): lax.all_to_all(outgoing.reshape((peers, capacity, length, width)), 'depth...]
    ppermute x13 -> x7, waiting for transfers between devices: 34.3 us -> 39 us  [shifted(): return lax.ppermute(value, axis, route)]
  transfers between devices with their start and end apart: 15 -> 9, of which waited for: 2 -> 3; matrix products, arithmetic and copies ran while one was open for 8% -> 4% of each run, Pallas kernels for 0% -> 13%
where the time goes in v1:
time: 303 us; the launch traced here: 302 us
  waiting for transfers between devices  171 us (56%)
  Pallas kernels  52.4 us (17%)
  starting transfers between devices  50.5 us (17%)
  local copies, waits for them, and re-layouts  14.6 us (5%)
  other arithmetic  6.85 us (2%)
  between operations  6.54 us (2%)
    all_to_all x1, waiting for transfers between devices, body(): lax.all_to_all(outgoing.reshape((peers, capacity, length, width)), 'depth...  132 us
    pallas_call x1, Pallas kernels, spread(): pl.pallas_call(spread_kernel, out_shape=jax.ShapeDtypeStruct((slot_count,...  39.3 us
    ppermute x7, waiting for transfers between devices, shifted(): return lax.ppermute(value, axis, route)  39 us
    ppermute x7, starting transfers between devices, shifted(): return lax.ppermute(value, axis, route)  21.2 us
    all_to_all x1, starting transfers between devices, body(): lax.all_to_all(outgoing.reshape((peers, capacity, length, width)), 'depth...  17 us
    all_to_all x1, starting transfers between devices, body(): lax.all_to_all(jnp.broadcast_to(targets[None], (peers, row_count)), 'dept...  12.2 us
    unnamed x23, local copies, waits for them, and re-layouts  8.95 us
    pallas_call x1, Pallas kernels, front(): pl.pallas_call(front_kernel, out_shape=(jax.ShapeDtypeStruct((tokens, wid...  8.83 us
  transfers between devices with their start and end apart: 9, of which 3 were waited for; matrix products, arithmetic and copies ran while one was open for 4% of the time, Pallas kernels for 13%

profile of v1, /device:TPU:2, one launch (start us, length us, event | category | flops | bytes accessed | tf_op | source)
XLA Modules:
  0.0 302.2 jit_solution(9487165566607872618)
XLA Ops:
  0.0 1.3 broadcast_in_dim.24
  1.3 12.2 %all-to-all-start = ((s32[64,1,32]{2,1,0:T(1,128)}), s32[64,1,32]{2,1,0:T(1,128)}, u32[]{:S(2)}, u32[]{:S(2)}) async-start(s32[64,1,32]{2,1,0:T(1,128)} %broadcast_in_dim.24), calls=%async_computation | async-start | bytes 65536 | tf_op jit(solution)/shard_map/all_to_all | solution.py:287
  13.5 1.2 compare_select_fusion.slot_ref
  14.7 39.3 %shard_map.76 = bf16[128,32,768]{2,1,0:T(8,128)(2,1)} custom-call(s32[32]{0:T(128)} %compare_select_fusion.slot_ref, bf16[32,32,768]{2,1,0:T(8,128)(2,1)} %bitcast.20), custom_call_target="tpu_custom_call" | custom-call | tf_op jit(solution)/shard_map/pallas_call | solution.py:41
  54.1 17.0 %all-to-all-start.1 = ((bf16[64,2,32,768]{3,2,1,0:T(8,128)(2,1)}), bf16[64,2,32,768]{3,2,1,0:T(8,128)(2,1)}, u32[]{:S(2)}, u32[]{:S(2)}) async-start(bf16[64,2,32,768]{3,2,1,0:T(8,128)(2,1)} %bitcast.19), calls=%async_computation.1 | async-start | bytes 12582912 | tf_op jit(solution)/shard_map/all_to_all | solution.py:280
  71.8 1.4 add.41
  73.9 1.5 subtract_reduce_fusion
  75.3 1.4 sub.45
  78.3 132.3 %all-to-all-done.1 = bf16[64,2,32,768]{3,2,1,0:T(8,128)(2,1)} async-done(((bf16[64,2,32,768]{3,2,1,0:T(8,128)(2,1)}), bf16[64,2,32,768]{3,2,1,0:T(8,128)(2,1)}, u32[]{:S(2)}, u32[]{:S(2)}) %all-to-all-start.1) | async-done | bytes 6291488 | tf_op jit(solution)/shard_map/all_to_all | solution.py:280
  210.6 8.8 %shard_map.77 = (bf16[1024,768]{1,0:T(8,128)(2,1)S(1)}, bf16[1024,768]{1,0:T(8,128)(2,1)S(1)}, f32[96,128]{1,0:T(8,128)S(1)}, bf16[96,128]{1,0:T(8,128)(2,1)}) custom-call(s32[32]{0:T(128)S(1)} %select_reduce_fusion.source_ref, bf16[128,32,768]{2,1,0:T(8,128)(2,1)} %bitcast.11.rows_ref, f32[1,768]{1,0:T(1,128)S(1)} %copy-done.8, f32[1,768]{1,0:T(1,128)S(1)} %copy-done.9, ...), custom_call_target="tpu_custom_call" | custom-call | tf_op jit(solution)/shard_map/pallas_call | solution.py:147
  222.4 4.3 %collective-permute-start.5 = (bf16[96,128]{1,0:T(8,128)(2,1)}, bf16[96,128]{1,0:T(8,128)(2,1)S(1)}, u32[]{:S(2)}, u32[]{:S(2)}) collective-permute-start(bf16[96,128]{1,0:T(8,128)(2,1)} %get-tuple-element.12), channel_id=1, source_target_pairs={{3,0},{4,1},{5,2},{6,3},{7,4},{8,5},{9,6},{10,7},{11,8},{12,9},{13... | collective-permute-start | bytes 73736 | tf_op jit(solution)/shard_map/ppermute | solution.py:255
  226.7 1.3 fusion.1
  234.4 1.9 collective-permute-start.4
  236.3 4.6 %collective-permute-start.3 = (bf16[96,128]{1,0:T(8,128)(2,1)}, bf16[96,128]{1,0:T(8,128)(2,1)S(1)}, u32[]{:S(2)}, u32[]{:S(2)}) collective-permute-start(bf16[96,128]{1,0:T(8,128)(2,1)} %get-tuple-element.12), channel_id=1, source_target_pairs={{2,0},{3,1},{4,2},{5,3},{6,4},{7,5},{8,6},{9,7},{10,8},{11,9},{12,... | collective-permute-start | bytes 73736 | tf_op jit(solution)/shard_map/ppermute | solution.py:255
  240.9 1.9 collective-permute-start.2
  242.8 5.1 %collective-permute-start.1 = (bf16[96,128]{1,0:T(8,128)(2,1)}, bf16[96,128]{1,0:T(8,128)(2,1)S(1)}, u32[]{:S(2)}, u32[]{:S(2)}) collective-permute-start(bf16[96,128]{1,0:T(8,128)(2,1)} %get-tuple-element.12), channel_id=1, source_target_pairs={{1,0},{2,1},{3,2},{4,3},{5,4},{6,5},{7,6},{8,7},{9,8},{10,9},{11,1... | collective-permute-start | bytes 73736 | tf_op jit(solution)/shard_map/ppermute | solution.py:255
  247.9 2.1 collective-permute-start
  251.5 3.8 %collective-permute-done.n1_ref = bf16[96,128]{1,0:T(8,128)(2,1)S(1)} collective-permute-done((bf16[96,128]{1,0:T(8,128)(2,1)}, bf16[96,128]{1,0:T(8,128)(2,1)S(1)}, u32[]{:S(2)}, u32[]{:S(2)}) %collective-permute-start) | collective-permute-done | bytes 24608 | tf_op jit(solution)/shard_map/ppermute | solution.py:255
  255.4 1.4 copy-done.2
  256.8 1.4 copy-done.4
  258.2 1.3 copy-done.5
  260.3 4.3 %shard_map.78 = bf16[1024,768]{1,0:T(8,128)(2,1)S(1)} custom-call(s32[32]{0:T(128)S(1)} %select_reduce_fusion.source_ref, f32[7]{0:T(128)S(1)} %stack.55.flag_ref, bf16[1024,768]{1,0:T(8,128)(2,1)S(1)} %copy-done.2, bf16[1024,768]{1,0:T(8,128)(2,1)S(1)} %copy-done.4, f32[96,128]{1,0:T(8,128)S(1)} %copy-done.7, ...), custom_call_target="tpu_custom_call" | custom-call | tf_op jit(solution)/shard_map/pallas_call | solution.py:239
  264.6 1.3 collective-permute-start.6
  265.9 35.2 %collective-permute-done.6 = bf16[1,32,32,768]{3,2,1,0:T(8,128)(2,1)S(1)} collective-permute-done((bf16[1,32,32,768]{3,2,1,0:T(8,128)(2,1)S(1)}, bf16[1,32,32,768]{3,2,1,0:T(8,128)(2,1)S(1)}, u32[]{:S(2)}, u32[]{:S(2)}) %collective-permute-start.6) | collective-permute-done | bytes 1572896 | tf_op jit(solution)/shard_map/ppermute | solution.py:255
  (36 shorter events, 9.3 us)
Async XLA Ops:
  1.3 52.7 %all-to-all-start = ((s32[64,1,32]{2,1,0:T(1,128)}), s32[64,1,32]{2,1,0:T(1,128)}, u32[]{:S(2)}, u32[]{:S(2)}) async-start(s32[64,1,32]{2,1,0:T(1,128)} %broadcast_in_dim.24), calls=%async_computation | async-start | bytes 65536 | tf_op jit(solution)/shard_map/all_to_all | solution.py:287
  54.0 19.3 %copy-start.10 = (s32[1,64]{1,0:T(1,128)S(1)}, s32[1,64]{1,0:T(1,128)}, u32[]{:S(2)}) copy-start(s32[1,64]{1,0:T(1,128)} %param.9) | copy-start | bytes 772
  54.0 156.6 %copy-start = (bf16[1,768,2304]{2,1,0:T(8,128)(2,1)S(1)}, bf16[1,768,2304]{2,1,0:T(8,128)(2,1)}, u32[]{:S(2)}) copy-start(bf16[1,768,2304]{2,1,0:T(8,128)(2,1)} %param.12) | copy-start | bytes 10616836
  54.0 156.6 %copy-start.8 = (f32[1,768]{1,0:T(1,128)S(1)}, f32[1,768]{1,0:T(1,128)}, u32[]{:S(2)}) copy-start(f32[1,768]{1,0:T(1,128)} %gain_ref.1) | copy-start | bytes 9220
  54.0 156.6 %copy-start.9 = (f32[1,768]{1,0:T(1,128)S(1)}, f32[1,768]{1,0:T(1,128)}, u32[]{:S(2)}) copy-start(f32[1,768]{1,0:T(1,128)} %bias_ref.1) | copy-start | bytes 9220
  54.1 156.6 %all-to-all-start.1 = ((bf16[64,2,32,768]{3,2,1,0:T(8,128)(2,1)}), bf16[64,2,32,768]{3,2,1,0:T(8,128)(2,1)}, u32[]{:S(2)}, u32[]{:S(2)}) async-start(bf16[64,2,32,768]{3,2,1,0:T(8,128)(2,1)} %bitcast.19), calls=%async_computation.1 | async-start | bytes 12582912 | tf_op jit(solution)/shard_map/all_to_all | solution.py:280
  219.5 1.1 copy-start.1
  220.6 1.2 copy-start.3
  221.8 0.6 copy-start.6
  222.4 25.5 %collective-permute-start.5 = (bf16[96,128]{1,0:T(8,128)(2,1)}, bf16[96,128]{1,0:T(8,128)(2,1)S(1)}, u32[]{:S(2)}, u32[]{:S(2)}) collective-permute-start(bf16[96,128]{1,0:T(8,128)(2,1)} %get-tuple-element.12), channel_id=1, source_target_pairs={{3,0},{4,1},{5,2},{6,3},{7,4},{8,5},{9,6},{10,7},{11,8},{12,9},{13... | collective-permute-start | bytes 73736 | tf_op jit(solution)/shard_map/ppermute | solution.py:255
  234.4 17.1 %collective-permute-start.4 = (bf16[96,128]{1,0:T(8,128)(2,1)}, bf16[96,128]{1,0:T(8,128)(2,1)S(1)}, u32[]{:S(2)}, u32[]{:S(2)}) collective-permute-start(bf16[96,128]{1,0:T(8,128)(2,1)} %get-tuple-element.12), channel_id=1, source_target_pairs={{0,3},{1,4},{2,5},{3,6},{4,7},{5,8},{6,9},{7,10},{8,11},{9,12},{10... | collective-permute-start | bytes 73736 | tf_op jit(solution)/shard_map/ppermute | solution.py:255
  236.3 15.2 %collective-permute-start.3 = (bf16[96,128]{1,0:T(8,128)(2,1)}, bf16[96,128]{1,0:T(8,128)(2,1)S(1)}, u32[]{:S(2)}, u32[]{:S(2)}) collective-permute-start(bf16[96,128]{1,0:T(8,128)(2,1)} %get-tuple-element.12), channel_id=1, source_target_pairs={{2,0},{3,1},{4,2},{5,3},{6,4},{7,5},{8,6},{9,7},{10,8},{11,9},{12,... | collective-permute-start | bytes 73736 | tf_op jit(solution)/shard_map/ppermute | solution.py:255
  240.9 10.6 %collective-permute-start.2 = (bf16[96,128]{1,0:T(8,128)(2,1)}, bf16[96,128]{1,0:T(8,128)(2,1)S(1)}, u32[]{:S(2)}, u32[]{:S(2)}) collective-permute-start(bf16[96,128]{1,0:T(8,128)(2,1)} %get-tuple-element.12), channel_id=1, source_target_pairs={{0,2},{1,3},{2,4},{3,5},{4,6},{5,7},{6,8},{7,9},{8,10},{9,11},{10,... | collective-permute-start | bytes 73736 | tf_op jit(solution)/shard_map/ppermute | solution.py:255
  242.8 8.7 %collective-permute-start.1 = (bf16[96,128]{1,0:T(8,128)(2,1)}, bf16[96,128]{1,0:T(8,128)(2,1)S(1)}, u32[]{:S(2)}, u32[]{:S(2)}) collective-permute-start(bf16[96,128]{1,0:T(8,128)(2,1)} %get-tuple-element.12), channel_id=1, source_target_pairs={{1,0},{2,1},{3,2},{4,3},{5,4},{6,5},{7,6},{8,7},{9,8},{10,9},{11,1... | collective-permute-start | bytes 73736 | tf_op jit(solution)/shard_map/ppermute | solution.py:255
  247.9 7.5 %collective-permute-start = (bf16[96,128]{1,0:T(8,128)(2,1)}, bf16[96,128]{1,0:T(8,128)(2,1)S(1)}, u32[]{:S(2)}, u32[]{:S(2)}) collective-permute-start(bf16[96,128]{1,0:T(8,128)(2,1)} %get-tuple-element.12), channel_id=1, source_target_pairs={{0,1},{1,2},{2,3},{3,4},{4,5},{5,6},{6,7},{7,8},{8,9},{9,10},{10,1... | collective-permute-start | bytes 73736 | tf_op jit(solution)/shard_map/ppermute | solution.py:255
  255.4 1.4 copy-start.2
  256.8 1.4 copy-start.4
  258.2 1.3 copy-start.5
  259.5 0.8 copy-start.7
  264.6 36.5 %collective-permute-start.6 = (bf16[1,32,32,768]{3,2,1,0:T(8,128)(2,1)S(1)}, bf16[1,32,32,768]{3,2,1,0:T(8,128)(2,1)S(1)}, u32[]{:S(2)}, u32[]{:S(2)}) collective-permute-start(bf16[1,32,32,768]{3,2,1,0:T(8,128)(2,1)S(1)} %bitcast.17), channel_id=1, source_target_pairs={{0,64},{64,128},{128,192},{192,0},{1,65},{65,129},{129,193},{193,1... | collective-permute-start | bytes 4718600 | tf_op jit(solution)/shard_map/ppermute | solution.py:255

commit v2 on v1

v2 whole, which is shorter than its diff:
```python
import jax
import jax.numpy as jnp
from jax import lax
from jax.experimental import pallas as pl
from jax.experimental.pallas import tpu as pltpu
from jax.sharding import PartitionSpec as P


H = 12
DH = 64
SPAN = 4
PAIRS = H // 2
EPSILON = 1e-05
CHUNK_ROWS = 8
INTERPRET = False


def spread_kernel(slot_ref, rows_ref, out_ref, sem):
    count = rows_ref.shape[0]

    def copy_of(i):
        return pltpu.make_async_copy(
            rows_ref.at[i], out_ref.at[jnp.maximum(slot_ref[i], 0)], sem.at[i]
        )

    for i in range(count):

        @pl.when(slot_ref[i] >= 0)
        def _():
            copy_of(i).start()

    for i in range(count):

        @pl.when(slot_ref[i] >= 0)
        def _():
            copy_of(i).wait()


def spread(rows, slots, slot_count):
    return pl.pallas_call(
        spread_kernel,
        out_shape=jax.ShapeDtypeStruct((slot_count,) + rows.shape[1:], rows.dtype),
        in_specs=[
            pl.BlockSpec(memory_space=pltpu.SMEM),
            pl.BlockSpec(memory_space=pltpu.VMEM),
        ],
        out_specs=pl.BlockSpec(memory_space=pl.ANY),
        scratch_shapes=[pltpu.SemaphoreType.DMA((rows.shape[0],))],
        name="spread",
        interpret=INTERPRET,
    )(slots, rows)


def settle_kernel(source_ref, rows_ref, *refs):
    out_ref, landed, in_sem, out_sem = refs[-4:]
    row_count, length = landed.shape[:2]

    def arrival(m):
        return pltpu.make_async_copy(
            rows_ref.at[jnp.maximum(source_ref[m], 0)], landed.at[m], in_sem.at[m]
        )

    def leaving(m):
        return pltpu.make_async_copy(
            landed.at[m], out_ref.at[pl.ds(m * length, length), :], out_sem.at[m]
        )

    for m in range(row_count):
        arrival(m).start()
    for m in range(row_count):
        arrival(m).wait()

        @pl.when(source_ref[m] < 0)
        def _():
            landed[m] = jnp.zeros_like(landed[m])

        leaving(m).start()
    for m in range(row_count):
        leaving(m).wait()


def settle(source, rows, scalars, early):
    row_count = source.shape[0]
    length, width = rows.shape[1:]
    return pl.pallas_call(
        settle_kernel,
        out_shape=jax.ShapeDtypeStruct((row_count * length, width), rows.dtype),
        in_specs=[
            pl.BlockSpec(memory_space=pltpu.SMEM),
            pl.BlockSpec(memory_space=pl.ANY),
        ]
        + [pl.BlockSpec(memory_space=pltpu.SMEM)] * len(scalars)
        + [pl.BlockSpec(memory_space=pl.ANY)] * len(early),
        out_specs=pl.BlockSpec(memory_space=pl.ANY),
        scratch_shapes=[
            pltpu.VMEM((row_count, length, width), rows.dtype),
            pltpu.SemaphoreType.DMA((row_count,)),
            pltpu.SemaphoreType.DMA((row_count,)),
        ],
        name="settle",
        interpret=INTERPRET,
    )(source, rows, *scalars, *early)


def lane_mask(shape):
    return lax.broadcasted_iota(jnp.int32, shape, len(shape) - 1) % 128 < DH


def normalized(block, gain, bias):
    widened = block.astype(jnp.float32)
    average = jnp.mean(widened, axis=-1, keepdims=True)
    centred = widened - average
    spread_of = jnp.mean(centred * centred, axis=-1, keepdims=True)
    return (centred * lax.rsqrt(spread_of + EPSILON) * gain + bias).astype(jnp.bfloat16)


def front_kernel(
    source_ref,
    meta_ref,
    scale_ref,
    rows_ref,
    gain_ref,
    bias_ref,
    weight_ref,
    tied_ref,
    tied_low_ref,
    landed,
    acc,
    sem,
):
    row_count = source_ref.shape[0]
    width = rows_ref.shape[1]
    length = rows_ref.shape[0] // row_count
    span = CHUNK_ROWS * length
    chunks = row_count // CHUNK_ROWS
    copies = [
        pltpu.make_async_copy(rows_ref.at[pl.ds(c * span, span), :], landed.at[c], sem.at[c])
        for c in range(chunks)
    ]
    for copy in copies:
        copy.start()
    gain = gain_ref[...]
    bias = bias_ref[...]
    weight = weight_ref[:, : 2 * width]
    first = lane_mask((length, 256))
    for c in range(chunks):
        copies[c].wait()
        start = c * CHUNK_ROWS
        normed = normalized(landed[c], gain, bias)
        packed = jnp.dot(normed, weight, preferred_element_type=jnp.float32).astype(jnp.bfloat16)
        for pair in range(PAIRS):
            lanes = slice(pair * 128, pair * 128 + 128)
            key_lanes = slice(width + pair * 128, width + pair * 128 + 128)
            total = None
            for r in range(0, CHUNK_ROWS, 2):
                query_parts = []
                key_parts = []
                for k in (r, r + 1):
                    own = slice(k * length, (k + 1) * length)
                    query = packed[own, lanes]
                    query_parts.append(
                        jnp.where(source_ref[start + k] >= 0, query, jnp.zeros_like(query))
                    )
                    key_parts.append(packed[own, key_lanes])
                query = jnp.concatenate(query_parts, axis=1)
                key = jnp.concatenate(key_parts, axis=1)
                zero = jnp.zeros_like(query)
                both = jnp.concatenate(
                    [jnp.where(first, query, zero), jnp.where(first, zero, query)], axis=0
                )
                part = lax.dot_general(
                    both, key, (((1,), (1,)), ((), ())), preferred_element_type=jnp.float32
                )
                total = part if total is None else total + part
            own = pl.ds(pair * 2 * length, 2 * length)
            if c == 0:
                acc[own, :] = total
            else:
                acc[own, :] += total
    quarter = H * length // 4
    tied = jnp.concatenate([acc[pl.ds(q * quarter, quarter), :] for q in range(4)], axis=1)
    tied_ref[...] = tied
    tied_low_ref[...] = tied.astype(jnp.bfloat16)


def front(source, meta, scale, rows, gain, bias, weight):
    row_count = source.shape[0]
    width = rows.shape[1]
    length = rows.shape[0] // row_count
    quarter = H * length // 4
    vmem = pl.BlockSpec(memory_space=pltpu.VMEM)
    smem = pl.BlockSpec(memory_space=pltpu.SMEM)
    return pl.pallas_call(
        front_kernel,
        out_shape=(
            jax.ShapeDtypeStruct((quarter, 4 * length), jnp.float32),
            jax.ShapeDtypeStruct((quarter, 4 * length), jnp.bfloat16),
        ),
        in_specs=[smem, smem, smem, pl.BlockSpec(memory_space=pl.ANY), vmem, vmem, vmem],
        out_specs=(vmem, vmem),
        scratch_shapes=[
            pltpu.VMEM((row_count // CHUNK_ROWS, CHUNK_ROWS * length, width), jnp.bfloat16),
            pltpu.VMEM((H * length, length), jnp.float32),
            pltpu.SemaphoreType.DMA((row_count // CHUNK_ROWS,)),
        ],
        compiler_params=pltpu.CompilerParams(vmem_limit_bytes=40 << 20),
        name="front",
        interpret=INTERPRET,
    )(source, meta, scale, rows, gain, bias, weight)


STEPS = tuple(d for k in range(1, SPAN) for d in (k, -k))


def middle_kernel(source_ref, meta_ref, scale_ref, tied_ref, *refs):
    neighbours, out_ref = refs[:-1], refs[-1]
    length = source_ref.shape[0]
    tied = tied_ref[...]
    position, low, high = meta_ref[0], meta_ref[1], meta_ref[2]
    for d, ref in zip(STEPS, neighbours):
        member = jnp.logical_and(position - d >= low, position - d < high)
        tied = tied + jnp.where(member, ref[...].astype(jnp.float32), 0.0)
    quarter = tied.shape[0]
    scale = scale_ref[0]
    logits = (
        jnp.concatenate([tied[:, q * length : (q + 1) * length] for q in range(4)], axis=0) * scale
    )
    top = jnp.max(logits, axis=-1, keepdims=True)
    raised = jnp.exp(logits - top)
    attention = raised / jnp.sum(raised, axis=-1, keepdims=True)
    out_ref[pl.ds(0, quarter), :] = jnp.concatenate(
        [attention[q * quarter : (q + 1) * quarter] for q in range(4)], axis=1
    ).astype(jnp.bfloat16)
    lane = lax.broadcasted_iota(jnp.int32, (16, 4 * length), 1)
    live = jnp.zeros((16, 4 * length), jnp.float32)
    for m in range(source_ref.shape[0]):
        live = jnp.where(jnp.logical_and(lane == m, source_ref[m] >= 0), 1.0, live)
    out_ref[pl.ds(quarter, 16), :] = live.astype(jnp.bfloat16)


def middle(source, meta, scale, tied, neighbours):
    vmem = pl.BlockSpec(memory_space=pltpu.VMEM)
    smem = pl.BlockSpec(memory_space=pltpu.SMEM)
    return pl.pallas_call(
        middle_kernel,
        out_shape=jax.ShapeDtypeStruct((tied.shape[0] + 16, tied.shape[1]), jnp.bfloat16),
        in_specs=[smem, smem, smem] + [vmem] * (1 + len(neighbours)),
        out_specs=vmem,
        name="middle",
        interpret=INTERPRET,
    )(source, meta, scale, tied, *neighbours)


def back_kernel(
    attention_ref, rows_ref, affine_ref, value_weight_ref, weight_ref, out_ref, landed, ready,
    in_sem, out_sem,
):
    chunks = landed.shape[0]
    span, _ = landed.shape[1:]
    length = span // CHUNK_ROWS
    quarter = H * length // 4
    arrivals = [
        pltpu.make_async_copy(rows_ref.at[pl.ds(c * span, span), :], landed.at[c], in_sem.at[c])
        for c in range(chunks)
    ]
    leavings = [
        pltpu.make_async_copy(ready.at[c], out_ref.at[pl.ds(c * span, span), :], out_sem.at[c])
        for c in range(chunks)
    ]
    for copy in arrivals:
        copy.start()
    packed = attention_ref[pl.ds(0, quarter), :]
    attention = jnp.concatenate(
        [packed[:, q * length : (q + 1) * length] for q in range(4)], axis=0
    )
    live = attention_ref[pl.ds(quarter, 16), :].astype(jnp.float32)
    wide = jnp.concatenate([attention] * CHUNK_ROWS, axis=1)
    diagonal = (
        lax.broadcasted_iota(jnp.int32, (span, span), 0) // length
        == lax.broadcasted_iota(jnp.int32, (span, span), 1) // length
    )
    first = lane_mask((span, 128))
    mixers = []
    for h in range(H):
        tall = jnp.concatenate([wide[h * length : (h + 1) * length]] * CHUNK_ROWS, axis=0)
        mixers.append(jnp.where(diagonal, tall, jnp.zeros_like(tall)))
    gain = affine_ref[0:1, :]
    bias = affine_ref[1:2, :]
    value_weight = value_weight_ref[...]
    weight = weight_ref[...]
    for c in range(chunks):
        arrivals[c].wait()
        block = landed[c]
        values = jnp.dot(
            normalized(block, gain, bias), value_weight, preferred_element_type=jnp.float32
        ).astype(jnp.bfloat16)
        parts = []
        for pair in range(PAIRS):
            lanes = values[:, pair * 128 : pair * 128 + 128]
            low = jnp.dot(mixers[2 * pair], lanes, preferred_element_type=jnp.float32)
            high = jnp.dot(mixers[2 * pair + 1], lanes, preferred_element_type=jnp.float32)
            parts.append(jnp.where(first, low, high).astype(jnp.bfloat16))
        attended = jnp.concatenate(parts, axis=1)
        mixed = jnp.dot(attended, weight, preferred_element_type=jnp.float32)
        mixed = mixed + block.astype(jnp.float32)
        for k in range(CHUNK_ROWS):
            m = c * CHUNK_ROWS + k
            own = mixed[k * length : (k + 1) * length]
            ready[c, pl.ds(k * length, length), :] = (
                own * jnp.broadcast_to(live[0:1, m : m + 1], own.shape)
            ).astype(jnp.bfloat16)
        leavings[c].start()
    for copy in leavings:
        copy.wait()


def back(attention, rows, affine, value_weight, weight, row_count):
    vmem = pl.BlockSpec(memory_space=pltpu.VMEM)
    anywhere = pl.BlockSpec(memory_space=pl.ANY)
    width = rows.shape[1]
    chunks = row_count // CHUNK_ROWS
    span = rows.shape[0] // chunks
    return pl.pallas_call(
        back_kernel,
        out_shape=jax.ShapeDtypeStruct(rows.shape, jnp.bfloat16),
        in_specs=[vmem, anywhere, vmem, vmem, vmem],
        out_specs=anywhere,
        scratch_shapes=[
            pltpu.VMEM((chunks, span, width), jnp.bfloat16),
            pltpu.VMEM((chunks, span, width), jnp.bfloat16),
            pltpu.SemaphoreType.DMA((chunks,)),
            pltpu.SemaphoreType.DMA((chunks,)),
        ],
        compiler_params=pltpu.CompilerParams(vmem_limit_bytes=40 << 20),
        name="back",
        interpret=INTERPRET,
    )(attention, rows, affine, value_weight, weight)


def shifted(value, axis, steps, wrap):
    count = lax.axis_size(axis)
    if wrap:
        route = [(i, (i + steps) % count) for i in range(count)]
    else:
        route = [(i, i + steps) for i in range(count) if 0 <= i + steps < count]
    return lax.ppermute(value, axis, route)


def layer(
    alignment_input,
    target_slot,
    device_alignment,
    layer_norm_gain,
    layer_norm_bias,
    query_key_value_weight,
    output_weight,
):
    incoming = alignment_input[0]
    targets = target_slot[0]
    groups = device_alignment[0]
    row_count, length, width = incoming.shape
    peers = lax.axis_size("depth")
    position = lax.axis_index("depth")
    capacity = max(2, (row_count + peers - 1) // peers)
    slots = jnp.where(
        targets >= 0,
        targets // row_count * capacity + jnp.arange(row_count) % capacity,
        -1,
    )
    outgoing = spread(incoming, slots, peers * capacity)
    got = lax.all_to_all(
        outgoing.reshape((peers, capacity, length, width)),
        "depth",
        split_axis=0,
        concat_axis=0,
        tiled=True,
    ).reshape(peers * capacity, length, width)
    everywhere = targets.reshape(1, row_count)
    while everywhere.shape[0] < peers:
        held = everywhere.shape[0]
        passed = shifted(everywhere[: peers - held], "depth", held, True)
        everywhere = jnp.concatenate([everywhere, passed], axis=0)
    value_weight = shifted(query_key_value_weight[0, :, 2 * width :], "section", 1, True)
    out_weight = shifted(output_weight[0], "section", 1, True)
    affine = shifted(
        jnp.concatenate([layer_norm_gain, layer_norm_bias], axis=0), "section", 1, True
    )
    local = everywhere - position * row_count
    mine = jnp.logical_and(local >= 0, local < row_count)
    sender = (position - lax.broadcasted_iota(jnp.int32, (peers, row_count), 0)) % peers
    code = (
        sender * capacity
        + lax.broadcasted_iota(jnp.int32, (peers, row_count), 1) % capacity
    )
    wanted = jnp.where(mine, local, -1).reshape(1, -1)
    hit = jnp.arange(row_count)[:, None] == wanted
    source = jnp.max(jnp.where(hit, code.reshape(1, -1), -1), axis=1)
    own_group = groups[position]
    low = jnp.sum((groups < own_group).astype(jnp.int32))
    high = low + jnp.sum((groups == own_group).astype(jnp.int32))
    inside = jnp.logical_and(everywhere >= low * row_count, everywhere < high * row_count)
    depth_total = jnp.sum(inside.astype(jnp.float32))
    meta = jnp.stack([position, low, high])
    scale = (DH ** (-0.5) / jnp.sqrt(depth_total)).reshape(1)
    balanced = settle(source, got, (meta, scale), (value_weight, out_weight, affine))
    earlier = shifted(balanced, "section", 1, True)
    tied, tied_low = front(
        source,
        meta,
        scale,
        balanced,
        layer_norm_gain,
        layer_norm_bias,
        query_key_value_weight[0],
    )
    neighbours = [shifted(tied_low, "depth", d, False) for d in STEPS]
    attention = shifted(middle(source, meta, scale, tied, neighbours), "section", 1, True)
    handed = back(attention, earlier, affine, value_weight, out_weight, row_count)
    return handed.reshape(1, row_count, length, width)


def solution(mesh):
    placed = (
        P("section", "depth", None, None),
        P("section", "depth"),
        P("section", None),
        P("section", None),
        P("section", None),
        P("section", None, None),
        P("section", None, None),
    )
    return jax.shard_map(
        layer,
        mesh=mesh,
        in_specs=placed,
        out_specs=P("section", "depth", None, None),
        check_vma=False,
    )
```

time: 303 us -> 271 us (0.89)
  Pallas kernels: 52.4 us -> 24.6 us
  waiting for transfers between devices: 171 us -> 145 us
  local copies, waits for them, and re-layouts: 14.6 us -> 24.6 us
  other arithmetic: 6.85 us -> 16.1 us
  starting transfers between devices: 50.5 us -> 54.9 us
  between operations: 6.54 us -> 3.01 us
    all_to_all x2 -> x1, waiting for transfers between devices: 132 us -> 0.01 us  [layer(): lax.all_to_all(outgoing.reshape((peers, capacity, length, width)), 'depth...]
    ppermute x7 -> x17, waiting for transfers between devices: 39 us -> 145 us  [shifted(): return lax.ppermute(value, axis, route)]
    pallas_call x1, Pallas kernels: 39.3 us -> 2.78 us  [spread(): pl.pallas_call(spread_kernel, out_shape=jax.ShapeDtypeStruct((slot_count,...]
    ppermute x7 -> x17, starting transfers between devices: 21.2 us -> 42.4 us  [shifted(): return lax.ppermute(value, axis, route)]
    all_to_all x2 -> x1, starting transfers between devices: 29.3 us -> 12.5 us  [layer(): lax.all_to_all(outgoing.reshape((peers, capacity, length, width)), 'depth...]
    concatenate x0 -> x3, local copies, waits for them, and re-layouts: none -> 11.6 us  [layer(): everywhere = jnp.concatenate([everywhere, passed], axis=0)]
    pallas_call x2 -> x4, Pallas kernels: 13.2 us -> 21.8 us  [the longest x1 9.66 us: back(): pl.pallas_call(back_kernel, out_shape=jax.ShapeDtypeStruct(rows.shape, jn...]
    concatenate x0 -> x4, other arithmetic: none -> 4.35 us  [the longest x3 3.75 us: layer(): everywhere = jnp.concatenate([everywhere, passed], axis=0)]
  transfers between devices with their start and end apart: 9 -> 18, of which waited for: 3 -> 8; matrix products, arithmetic and copies ran while one was open for 4% -> 13% of each run, Pallas kernels for 13% -> 3%
where the time goes in v2:
time: 271 us; the launch traced here: 268 us
  waiting for transfers between devices  145 us (54%)
  starting transfers between devices  54.9 us (20%)
  Pallas kernels  24.6 us (9%)
  local copies, waits for them, and re-layouts  24.6 us (9%)
  other arithmetic  16.1 us (6%)
  between operations  3.01 us (1%)
    ppermute x17, waiting for transfers between devices, shifted(): return lax.ppermute(value, axis, route)  145 us
    ppermute x17, starting transfers between devices, shifted(): return lax.ppermute(value, axis, route)  42.4 us
    all_to_all x1, starting transfers between devices, layer(): lax.all_to_all(outgoing.reshape((peers, capacity, length, width)), 'depth...  12.5 us
    concatenate x3, local copies, waits for them, and re-layouts, layer(): everywhere = jnp.concatenate([everywhere, passed], axis=0)  11.6 us
    pallas_call x1, Pallas kernels, back(): pl.pallas_call(back_kernel, out_shape=jax.ShapeDtypeStruct(rows.shape, jn...  9.66 us
    pallas_call x1, Pallas kernels, front(): pl.pallas_call(front_kernel, out_shape=(jax.ShapeDtypeStruct((quarter, 4...  6.53 us
  transfers between devices with their start and end apart: 18, of which 8 were waited for; matrix products, arithmetic and copies ran while one was open for 13% of the time, Pallas kernels for 3%

profile of v2, /device:TPU:2, one launch (start us, length us, event | category | flops | bytes accessed | tf_op | source)
XLA Modules:
  0.0 268.0 jit_solution(982628367955421543)
XLA Ops:
  1.2 2.8 %spread.1 = bf16[128,32,768]{2,1,0:T(8,128)(2,1)} custom-call(s32[32]{0:T(128)} %compare_select_fusion.slot_ref, bf16[32,32,768]{2,1,0:T(8,128)(2,1)} %bitcast.26), custom_call_target="tpu_custom_call" | custom-call | tf_op jit(solution)/shard_map/spread/pallas_call | solution.py:40
  4.0 12.5 %all-to-all-start = ((bf16[64,2,32,768]{3,2,1,0:T(8,128)(2,1)}), bf16[64,2,32,768]{3,2,1,0:T(8,128)(2,1)}, u32[]{:S(2)}, u32[]{:S(2)}) async-start(bf16[64,2,32,768]{3,2,1,0:T(8,128)(2,1)} %bitcast.25), calls=%async_computation | async-start | bytes 12582912 | tf_op jit(solution)/shard_map/all_to_all | solution.py:371
  23.0 128.1 %collective-permute-done = s32[1,32]{1,0:T(1,128)S(1)} collective-permute-done((s32[1,32]{1,0:T(1,128)}, s32[1,32]{1,0:T(1,128)S(1)}, u32[]{:S(2)}, u32[]{:S(2)}) %collective-permute-start) | collective-permute-done | bytes 160 | tf_op jit(solution)/shard_map/ppermute | solution.py:346
  154.8 3.7 %collective-permute-done.1 = s32[2,32]{1,0:T(2,128)} collective-permute-done((s32[2,32]{1,0:T(2,128)}, s32[2,32]{1,0:T(2,128)}, u32[]{:S(2)}, u32[]{:S(2)}) %collective-permute-start.1) | collective-permute-done | bytes 288 | tf_op jit(solution)/shard_map/ppermute | solution.py:346
  167.8 3.0 %collective-permute-start.3 = (s32[8,32]{1,0:T(8,128)}, s32[8,32]{1,0:T(8,128)}, u32[]{:S(2)}, u32[]{:S(2)}) collective-permute-start(s32[8,32]{1,0:T(8,128)} %pad_add_fusion), channel_id=1, source_target_pairs={{0,8},{1,9},{2,10},{3,11},{4,12},{5,13},{6,14},{7,15},{8,16},{9,17... | collective-permute-start | bytes 3080 | tf_op jit(solution)/shard_map/ppermute | solution.py:346
  173.4 3.1 %collective-permute-done.3 = s32[8,32]{1,0:T(8,128)} collective-permute-done((s32[8,32]{1,0:T(8,128)}, s32[8,32]{1,0:T(8,128)}, u32[]{:S(2)}, u32[]{:S(2)}) %collective-permute-start.3) | collective-permute-done | bytes 1056 | tf_op jit(solution)/shard_map/ppermute | solution.py:346
  176.5 2.6 concatenate.29
  180.5 2.0 fusion.4
  183.8 3.8 %collective-permute-done.4 = s32[16,32]{1,0:T(8,128)} collective-permute-done((s32[16,32]{1,0:T(8,128)}, s32[16,32]{1,0:T(8,128)}, u32[]{:S(2)}, u32[]{:S(2)}) %collective-permute-start.4) | collective-permute-done | bytes 2080 | tf_op jit(solution)/shard_map/ppermute | solution.py:346
  187.5 3.9 %concatenate.30 = s32[32,32]{1,0:T(8,128)} concatenate(s32[1,32]{1,0:T(1,128)} %param.8, s32[1,32]{1,0:T(1,128)} %copy-done.15, s32[2,32]{1,0:T(2,128)} %collective-permute-done.1, s32[4,32]{1,0:T(4,128)} %collective-permute-done.2, s32[8,32]{1,0:T(8,128)} %collective-permute-done.3, s32[16,32]{1,0:T(8,128)} %collective-permute-done.4), dimensions={0} | concatenate | bytes 8192 | tf_op jit(solution)/shard_map/concatenate | solution.py:382
  191.4 3.4 %collective-permute-start.5 = (s32[32,32]{1,0:T(8,128)}, s32[32,32]{1,0:T(8,128)}, u32[]{:S(2)}, u32[]{:S(2)}) collective-permute-start(s32[32,32]{1,0:T(8,128)} %concatenate.30), channel_id=1, source_target_pairs={{0,32},{1,33},{2,34},{3,35},{4,36},{5,37},{6,38},{7,39},{8,40},{9,... | collective-permute-start | bytes 12296 | tf_op jit(solution)/shard_map/ppermute | solution.py:346
  197.0 5.2 %concatenate.31 = s32[64,32]{1,0:T(8,128)} concatenate(s32[1,32]{1,0:T(1,128)} %param.8, s32[1,32]{1,0:T(1,128)} %copy-done.15, s32[2,32]{1,0:T(2,128)} %collective-permute-done.1, s32[4,32]{1,0:T(4,128)} %collective-permute-done.2, s32[8,32]{1,0:T(8,128)} %collective-permute-done.3, s32[16,32]{1,0:T(8,128)} %collective-permute-done.4, s32[32,32]{1,0:T(8,128)} %collective-permute-done.5), dimensions={0} | concatenate | bytes 16384 | tf_op jit(solution)/shard_map/concatenate | solution.py:382
  209.7 3.8 %settle.1.rows_ref = bf16[1024,768]{1,0:T(8,128)(2,1)} custom-call(s32[32]{0:T(128)} %select_reduce_fusion.source_ref, bf16[128,32,768]{2,1,0:T(8,128)(2,1)} %bitcast.8.rows_ref, s32[3]{0:T(128)} %pad_add_fusion.3.refs_0_.meta_ref, f32[1]{0:T(128)} %bitcast.4.refs_1_.scale_ref, bf16[768,768]{1,0:T(8,128)(2,1)} %collective-permute-done.6.refs_2_.value_weight_ref, ...), custom_call_target="tpu_custom_call" | custom-call | tf_op jit(solution)/shard_map/settle/pallas_call | solution.py:85
  217.5 6.5 %front.1 = (f32[96,128]{1,0:T(8,128)S(1)}, bf16[96,128]{1,0:T(8,128)(2,1)S(1)}) custom-call(s32[32]{0:T(128)S(1)} %copy-done.7, s32[3]{0:T(128)S(1)} %copy-done.8, f32[1]{0:T(128)} %bitcast.4.refs_1_.scale_ref, bf16[1024,768]{1,0:T(8,128)(2,1)S(1)} %copy-done.1, f32[1,768]{1,0:T(1,128)S(1)} %copy-done.6, f32[1,768]{1,0:T(1,128)S(1)} %copy-done.5, ...), custom_call_target="tpu_custom_call" | custom-call | tf_op jit(solution)/shard_map/front/pallas_call | solution.py:193
  224.6 1.9 collective-permute-start.9
  226.6 5.8 %collective-permute-start.10 = (bf16[96,128]{1,0:T(8,128)(2,1)S(1)}, bf16[96,128]{1,0:T(8,128)(2,1)S(1)}, u32[]{:S(2)}, u32[]{:S(2)}) collective-permute-start(bf16[96,128]{1,0:T(8,128)(2,1)S(1)} %get-tuple-element.8), channel_id=1, source_target_pairs={{1,0},{2,1},{3,2},{4,3},{5,4},{6,5},{7,6},{8,7},{9,8},{10,9},{11,1... | collective-permute-start | bytes 73736 | tf_op jit(solution)/shard_map/ppermute | solution.py:346
  232.3 1.9 collective-permute-start.11
  234.2 6.0 %collective-permute-start.12 = (bf16[96,128]{1,0:T(8,128)(2,1)S(1)}, bf16[96,128]{1,0:T(8,128)(2,1)S(1)}, u32[]{:S(2)}, u32[]{:S(2)}) collective-permute-start(bf16[96,128]{1,0:T(8,128)(2,1)S(1)} %get-tuple-element.8), channel_id=1, source_target_pairs={{2,0},{3,1},{4,2},{5,3},{6,4},{7,5},{8,6},{9,7},{10,8},{11,9},{12,... | collective-permute-start | bytes 73736 | tf_op jit(solution)/shard_map/ppermute | solution.py:346
  240.3 1.9 collective-permute-start.13
  242.2 6.7 %collective-permute-start.14 = (bf16[96,128]{1,0:T(8,128)(2,1)S(1)}, bf16[96,128]{1,0:T(8,128)(2,1)S(1)}, u32[]{:S(2)}, u32[]{:S(2)}) collective-permute-start(bf16[96,128]{1,0:T(8,128)(2,1)S(1)} %get-tuple-element.8), channel_id=1, source_target_pairs={{3,0},{4,1},{5,2},{6,3},{7,4},{8,5},{9,6},{10,7},{11,8},{12,9},{13... | collective-permute-start | bytes 73736 | tf_op jit(solution)/shard_map/ppermute | solution.py:346
  251.0 1.8 middle.1
  252.8 2.1 collective-permute-start.15
  254.9 3.2 %collective-permute-done.15.attention_ref = bf16[112,128]{1,0:T(8,128)(2,1)S(1)} collective-permute-done((bf16[112,128]{1,0:T(8,128)(2,1)}, bf16[112,128]{1,0:T(8,128)(2,1)S(1)}, u32[]{:S(2)}, u32[]{:S(2)}) %collective-permute-start.15) | collective-permute-done | bytes 28704 | tf_op jit(solution)/shard_map/ppermute | solution.py:346
  258.1 9.7 %back.1 = bf16[1024,768]{1,0:T(8,128)(2,1)} custom-call(bf16[112,128]{1,0:T(8,128)(2,1)S(1)} %collective-permute-done.15.attention_ref, bf16[1024,768]{1,0:T(8,128)(2,1)} %collective-permute-done.16.rows_ref, f32[2,768]{1,0:T(2,128)S(1)} %copy-done.4, bf16[768,768]{1,0:T(8,128)(2,1)} %collective-permute-done.6.refs_2_.value_weight_ref, ...), custom_call_target="tpu_custom_call" | custom-call | tf_op jit(solution)/shard_map/back/pallas_call | solution.py:323
  (74 shorter events, 39.7 us)
Async XLA Ops:
  4.0 12.8 %copy-start = (bf16[1,768,2304]{2,1,0:T(8,128)(2,1)S(1)}, bf16[1,768,2304]{2,1,0:T(8,128)(2,1)}, u32[]{:S(2)}) copy-start(bf16[1,768,2304]{2,1,0:T(8,128)(2,1)} %param.12) | copy-start | bytes 10616836
  4.0 205.2 %all-to-all-start = ((bf16[64,2,32,768]{3,2,1,0:T(8,128)(2,1)}), bf16[64,2,32,768]{3,2,1,0:T(8,128)(2,1)}, u32[]{:S(2)}, u32[]{:S(2)}) async-start(bf16[64,2,32,768]{3,2,1,0:T(8,128)(2,1)} %bitcast.25), calls=%async_computation | async-start | bytes 12582912 | tf_op jit(solution)/shard_map/all_to_all | solution.py:371
  16.5 4.5 %copy-start.5 = (f32[1,768]{1,0:T(1,128)S(1)}, f32[1,768]{1,0:T(1,128)}, u32[]{:S(2)}) copy-start(f32[1,768]{1,0:T(1,128)} %bias_ref.1) | copy-start | bytes 9220
  16.5 4.5 %copy-start.6 = (f32[1,768]{1,0:T(1,128)S(1)}, f32[1,768]{1,0:T(1,128)}, u32[]{:S(2)}) copy-start(f32[1,768]{1,0:T(1,128)} %gain_ref.1) | copy-start | bytes 9220
  16.5 134.5 %collective-permute-start = (s32[1,32]{1,0:T(1,128)}, s32[1,32]{1,0:T(1,128)S(1)}, u32[]{:S(2)}, u32[]{:S(2)}) collective-permute-start(s32[1,32]{1,0:T(1,128)} %param.8), channel_id=1, source_target_pairs={{0,1},{1,2},{2,3},{3,4},{4,5},{5,6},{6,7},{7,8},{8,9},{9,10},{10,1... | collective-permute-start | bytes 392 | tf_op jit(solution)/shard_map/ppermute | solution.py:346
  17.8 191.3 %collective-permute-start.6 = (bf16[768,768]{1,0:T(8,128)(2,1)}, bf16[768,768]{1,0:T(8,128)(2,1)}, u32[]{:S(2)}, u32[]{:S(2)}) collective-permute-start(bf16[768,768]{1,0:T(8,128)(2,1)} %slice_bitcast_fusion), channel_id=1, source_target_pairs={{0,64},{64,128},{128,192},{192,0},{1,65},{65,129},{129,193},{193,1... | collective-permute-start | bytes 3538952 | tf_op jit(solution)/shard_map/ppermute | solution.py:346
  19.4 189.8 %collective-permute-start.7 = (bf16[768,768]{1,0:T(8,128)(2,1)}, bf16[768,768]{1,0:T(8,128)(2,1)}, u32[]{:S(2)}, u32[]{:S(2)}) collective-permute-start(bf16[768,768]{1,0:T(8,128)(2,1)} %bitcast.10), channel_id=1, source_target_pairs={{0,64},{64,128},{128,192},{192,0},{1,65},{65,129},{129,193},{193,1... | collective-permute-start | bytes 3538952 | tf_op jit(solution)/shard_map/ppermute | solution.py:346
  21.6 187.6 %collective-permute-start.8 = (f32[2,768]{1,0:T(2,128)}, f32[2,768]{1,0:T(2,128)S(1)}, u32[]{:S(2)}, u32[]{:S(2)}) collective-permute-start(f32[2,768]{1,0:T(2,128)} %pad_maximum_fusion), channel_id=1, source_target_pairs={{0,64},{64,128},{128,192},{192,0},{1,65},{65,129},{129,193},{193,1... | collective-permute-start | bytes 18440 | tf_op jit(solution)/shard_map/ppermute | solution.py:346
  152.8 5.7 %collective-permute-start.1 = (s32[2,32]{1,0:T(2,128)}, s32[2,32]{1,0:T(2,128)}, u32[]{:S(2)}, u32[]{:S(2)}) collective-permute-start(s32[2,32]{1,0:T(2,128)} %pad_add_fusion.2), channel_id=1, source_target_pairs={{0,2},{1,3},{2,4},{3,5},{4,6},{5,7},{6,8},{7,9},{8,10},{9,11},{10,... | collective-permute-start | bytes 776 | tf_op jit(solution)/shard_map/ppermute | solution.py:346
  159.7 6.8 %collective-permute-start.2 = (s32[4,32]{1,0:T(4,128)}, s32[4,32]{1,0:T(4,128)}, u32[]{:S(2)}, u32[]{:S(2)}) collective-permute-start(s32[4,32]{1,0:T(4,128)} %pad_add_fusion.1), channel_id=1, source_target_pairs={{0,4},{1,5},{2,6},{3,7},{4,8},{5,9},{6,10},{7,11},{8,12},{9,13},{1... | collective-permute-start | bytes 1544 | tf_op jit(solution)/shard_map/ppermute | solution.py:346
  167.8 8.7 %collective-permute-start.3 = (s32[8,32]{1,0:T(8,128)}, s32[8,32]{1,0:T(8,128)}, u32[]{:S(2)}, u32[]{:S(2)}) collective-permute-start(s32[8,32]{1,0:T(8,128)} %pad_add_fusion), channel_id=1, source_target_pairs={{0,8},{1,9},{2,10},{3,11},{4,12},{5,13},{6,14},{7,15},{8,16},{9,17... | collective-permute-start | bytes 3080 | tf_op jit(solution)/shard_map/ppermute | solution.py:346
  179.1 8.5 %collective-permute-start.4 = (s32[16,32]{1,0:T(8,128)}, s32[16,32]{1,0:T(8,128)}, u32[]{:S(2)}, u32[]{:S(2)}) collective-permute-start(s32[16,32]{1,0:T(8,128)} %concatenate.29), channel_id=1, source_target_pairs={{0,16},{1,17},{2,18},{3,19},{4,20},{5,21},{6,22},{7,23},{8,24},{9,... | collective-permute-start | bytes 6152 | tf_op jit(solution)/shard_map/ppermute | solution.py:346
  191.4 5.6 %collective-permute-start.5 = (s32[32,32]{1,0:T(8,128)}, s32[32,32]{1,0:T(8,128)}, u32[]{:S(2)}, u32[]{:S(2)}) collective-permute-start(s32[32,32]{1,0:T(8,128)} %concatenate.30), channel_id=1, source_target_pairs={{0,32},{1,33},{2,34},{3,35},{4,36},{5,37},{6,38},{7,39},{8,40},{9,... | collective-permute-start | bytes 12296 | tf_op jit(solution)/shard_map/ppermute | solution.py:346
  213.5 44.6 %collective-permute-start.16 = (bf16[1024,768]{1,0:T(8,128)(2,1)}, bf16[1024,768]{1,0:T(8,128)(2,1)}, u32[]{:S(2)}, u32[]{:S(2)}) collective-permute-start(bf16[1024,768]{1,0:T(8,128)(2,1)} %settle.1.rows_ref), channel_id=1, source_target_pairs={{0,64},{64,128},{128,192},{192,0},{1,65},{65,129},{129,193},{193,1... | collective-permute-start | bytes 4718600 | tf_op jit(solution)/shard_map/ppermute | solution.py:346
  217.5 40.7 %copy-start.4 = (f32[2,768]{1,0:T(2,128)S(1)}, f32[2,768]{1,0:T(2,128)}, u32[]{:S(2)}) copy-start(f32[2,768]{1,0:T(2,128)} %copy-done.3) | copy-start | bytes 18436
  224.6 15.6 %collective-permute-start.9 = (bf16[96,128]{1,0:T(8,128)(2,1)S(1)}, bf16[96,128]{1,0:T(8,128)(2,1)S(1)}, u32[]{:S(2)}, u32[]{:S(2)}) collective-permute-start(bf16[96,128]{1,0:T(8,128)(2,1)S(1)} %get-tuple-element.8), channel_id=1, source_target_pairs={{0,1},{1,2},{2,3},{3,4},{4,5},{5,6},{6,7},{7,8},{8,9},{9,10},{10,1... | collective-permute-start | bytes 73736 | tf_op jit(solution)/shard_map/ppermute | solution.py:346
  226.6 15.7 %collective-permute-start.10 = (bf16[96,128]{1,0:T(8,128)(2,1)S(1)}, bf16[96,128]{1,0:T(8,128)(2,1)S(1)}, u32[]{:S(2)}, u32[]{:S(2)}) collective-permute-start(bf16[96,128]{1,0:T(8,128)(2,1)S(1)} %get-tuple-element.8), channel_id=1, source_target_pairs={{1,0},{2,1},{3,2},{4,3},{5,4},{6,5},{7,6},{8,7},{9,8},{10,9},{11,1... | collective-permute-start | bytes 73736 | tf_op jit(solution)/shard_map/ppermute | solution.py:346
  232.3 16.6 %collective-permute-start.11 = (bf16[96,128]{1,0:T(8,128)(2,1)S(1)}, bf16[96,128]{1,0:T(8,128)(2,1)S(1)}, u32[]{:S(2)}, u32[]{:S(2)}) collective-permute-start(bf16[96,128]{1,0:T(8,128)(2,1)S(1)} %get-tuple-element.8), channel_id=1, source_target_pairs={{0,2},{1,3},{2,4},{3,5},{4,6},{5,7},{6,8},{7,9},{8,10},{9,11},{10,... | collective-permute-start | bytes 73736 | tf_op jit(solution)/shard_map/ppermute | solution.py:346
  234.2 14.7 %collective-permute-start.12 = (bf16[96,128]{1,0:T(8,128)(2,1)S(1)}, bf16[96,128]{1,0:T(8,128)(2,1)S(1)}, u32[]{:S(2)}, u32[]{:S(2)}) collective-permute-start(bf16[96,128]{1,0:T(8,128)(2,1)S(1)} %get-tuple-element.8), channel_id=1, source_target_pairs={{2,0},{3,1},{4,2},{5,3},{6,4},{7,5},{8,6},{9,7},{10,8},{11,9},{12,... | collective-permute-start | bytes 73736 | tf_op jit(solution)/shard_map/ppermute | solution.py:346
  240.3 10.1 %copy-start.9 = (bf16[96,128]{1,0:T(8,128)(2,1)}, bf16[96,128]{1,0:T(8,128)(2,1)S(1)}, u32[]{:S(2)}) copy-start(bf16[96,128]{1,0:T(8,128)(2,1)S(1)} %collective-permute-done.9.refs_0_) | copy-start | bytes 73732
  240.3 8.7 %collective-permute-start.13 = (bf16[96,128]{1,0:T(8,128)(2,1)S(1)}, bf16[96,128]{1,0:T(8,128)(2,1)S(1)}, u32[]{:S(2)}, u32[]{:S(2)}) collective-permute-start(bf16[96,128]{1,0:T(8,128)(2,1)S(1)} %get-tuple-element.8), channel_id=1, source_target_pairs={{0,3},{1,4},{2,5},{3,6},{4,7},{5,8},{6,9},{7,10},{8,11},{9,12},{10... | collective-permute-start | bytes 73736 | tf_op jit(solution)/shard_map/ppermute | solution.py:346
  242.2 8.2 %copy-start.10 = (bf16[96,128]{1,0:T(8,128)(2,1)}, bf16[96,128]{1,0:T(8,128)(2,1)S(1)}, u32[]{:S(2)}) copy-start(bf16[96,128]{1,0:T(8,128)(2,1)S(1)} %collective-permute-done.10.refs_1_) | copy-start | bytes 73732
  242.2 8.2 %collective-permute-start.14 = (bf16[96,128]{1,0:T(8,128)(2,1)S(1)}, bf16[96,128]{1,0:T(8,128)(2,1)S(1)}, u32[]{:S(2)}, u32[]{:S(2)}) collective-permute-start(bf16[96,128]{1,0:T(8,128)(2,1)S(1)} %get-tuple-element.8), channel_id=1, source_target_pairs={{3,0},{4,1},{5,2},{6,3},{7,4},{8,5},{9,6},{10,7},{11,8},{12,9},{13... | collective-permute-start | bytes 73736 | tf_op jit(solution)/shard_map/ppermute | solution.py:346
  252.8 5.3 %collective-permute-start.15 = (bf16[112,128]{1,0:T(8,128)(2,1)}, bf16[112,128]{1,0:T(8,128)(2,1)S(1)}, u32[]{:S(2)}, u32[]{:S(2)}) collective-permute-start(bf16[112,128]{1,0:T(8,128)(2,1)} %middle.1), channel_id=1, source_target_pairs={{0,64},{64,128},{128,192},{192,0},{1,65},{65,129},{129,193},{193,1... | collective-permute-start | bytes 86024 | tf_op jit(solution)/shard_map/ppermute | solution.py:346
  (10 other events, 9.5 us)

commit v3 on v2

--- a/solution.py
+++ b/solution.py
@@ -44,7 +44,7 @@
             pl.BlockSpec(memory_space=pltpu.SMEM),
             pl.BlockSpec(memory_space=pltpu.VMEM),
         ],
-        out_specs=pl.BlockSpec(memory_space=pl.ANY),
+        out_specs=pl.BlockSpec(memory_space=pltpu.HBM),
         scratch_shapes=[pltpu.SemaphoreType.DMA((rows.shape[0],))],
         name="spread",
         interpret=INTERPRET,
@@ -91,7 +91,7 @@
         ]
         + [pl.BlockSpec(memory_space=pltpu.SMEM)] * len(scalars)
         + [pl.BlockSpec(memory_space=pl.ANY)] * len(early),
-        out_specs=pl.BlockSpec(memory_space=pl.ANY),
+        out_specs=pl.BlockSpec(memory_space=pltpu.HBM),
         scratch_shapes=[
             pltpu.VMEM((row_count, length, width), rows.dtype),
             pltpu.SemaphoreType.DMA((row_count,)),
@@ -196,7 +196,7 @@
             jax.ShapeDtypeStruct((quarter, 4 * length), jnp.float32),
             jax.ShapeDtypeStruct((quarter, 4 * length), jnp.bfloat16),
         ),
-        in_specs=[smem, smem, smem, pl.BlockSpec(memory_space=pl.ANY), vmem, vmem, vmem],
+        in_specs=[smem, smem, smem, pl.BlockSpec(memory_space=pltpu.HBM), vmem, vmem, vmem],
         out_specs=(vmem, vmem),
         scratch_shapes=[
             pltpu.VMEM((row_count // CHUNK_ROWS, CHUNK_ROWS * length, width), jnp.bfloat16),
@@ -316,7 +316,7 @@
 
 def back(attention, rows, affine, value_weight, weight, row_count):
     vmem = pl.BlockSpec(memory_space=pltpu.VMEM)
-    anywhere = pl.BlockSpec(memory_space=pl.ANY)
+    anywhere = pl.BlockSpec(memory_space=pltpu.HBM)
     width = rows.shape[1]
     chunks = row_count // CHUNK_ROWS
     span = rows.shape[0] // chunks
@@ -375,11 +375,13 @@
         concat_axis=0,
         tiled=True,
     ).reshape(peers * capacity, length, width)
-    everywhere = targets.reshape(1, row_count)
-    while everywhere.shape[0] < peers:
-        held = everywhere.shape[0]
-        passed = shifted(everywhere[: peers - held], "depth", held, True)
-        everywhere = jnp.concatenate([everywhere, passed], axis=0)
+    everywhere = lax.all_to_all(
+        jnp.broadcast_to(targets[None, None], (peers, 1, row_count)),
+        "depth",
+        split_axis=0,
+        concat_axis=0,
+        tiled=True,
+    ).reshape(peers, row_count)
     value_weight = shifted(query_key_value_weight[0, :, 2 * width :], "section", 1, True)
     out_weight = shifted(output_weight[0], "section", 1, True)
     affine = shifted(
@@ -387,7 +389,7 @@
     )
     local = everywhere - position * row_count
     mine = jnp.logical_and(local >= 0, local < row_count)
-    sender = (position - lax.broadcasted_iota(jnp.int32, (peers, row_count), 0)) % peers
+    sender = lax.broadcasted_iota(jnp.int32, (peers, row_count), 0)
     code = (
         sender * capacity
         + lax.broadcasted_iota(jnp.int32, (peers, row_count), 1) % capacity

time: 271 us -> 228 us (0.84)
  waiting for transfers between devices: 145 us -> 125 us
  local copies, waits for them, and re-layouts: 24.6 us -> 12.6 us
  other arithmetic: 16.1 us -> 10.8 us
  starting transfers between devices: 54.9 us -> 50.6 us
    ppermute x17 -> x11, waiting for transfers between devices: 145 us -> 37.5 us  [shifted(): return lax.ppermute(value, axis, route)]
    all_to_all x1, waiting for transfers between devices: 0.01 us -> 83.5 us  [layer(): lax.all_to_all(outgoing.reshape((peers, capacity, length, width)), 'depth...]
    all_to_all x0 -> x1, starting transfers between devices: none -> 12 us  [layer(): lax.all_to_all(jnp.broadcast_to(targets[None, None], (peers, 1, row_count...]
    concatenate x3 -> x0, local copies, waits for them, and re-layouts: 11.6 us -> none  [layer(): everywhere = jnp.concatenate([everywhere, passed], axis=0)]
    ppermute x17 -> x11, starting transfers between devices: 42.4 us -> 31.8 us  [shifted(): return lax.ppermute(value, axis, route)]
    all_to_all x1, starting transfers between devices: 12.5 us -> 6.78 us  [layer(): lax.all_to_all(outgoing.reshape((peers, capacity, length, width)), 'depth...]
    all_to_all x0 -> x1, waiting for transfers between devices: none -> 4.53 us  [layer(): lax.all_to_all(jnp.broadcast_to(targets[None, None], (peers, 1, row_count...]
    concatenate x3 -> x0, other arithmetic: 3.75 us -> none  [layer(): everywhere = jnp.concatenate([everywhere, passed], axis=0)]
  transfers between devices with their start and end apart: 18 -> 13, of which waited for: 8 -> 5; matrix products, arithmetic and copies ran while one was open for 13% -> 8% of each run, Pallas kernels for 3% -> 5%
where the time goes in v3:
time: 228 us; the launch traced here: 227 us
  waiting for transfers between devices  125 us (55%)
  starting transfers between devices  50.6 us (22%)
  Pallas kernels  24.5 us (11%)
  local copies, waits for them, and re-layouts  12.6 us (6%)
  other arithmetic  10.8 us (5%)
  between operations  3 us (1%)
    all_to_all x1, waiting for transfers between devices, layer(): lax.all_to_all(outgoing.reshape((peers, capacity, length, width)), 'depth...  83.5 us
    ppermute x11, waiting for transfers between devices, shifted(): return lax.ppermute(value, axis, route)  37.5 us
    ppermute x11, starting transfers between devices, shifted(): return lax.ppermute(value, axis, route)  31.8 us
    all_to_all x1, starting transfers between devices, layer(): lax.all_to_all(jnp.broadcast_to(targets[None, None], (peers, 1, row_count...  12 us
    pallas_call x1, Pallas kernels, back(): pl.pallas_call(back_kernel, out_shape=jax.ShapeDtypeStruct(rows.shape, jn...  9.66 us
    all_to_all x1, starting transfers between devices, layer(): lax.all_to_all(outgoing.reshape((peers, capacity, length, width)), 'depth...  6.78 us
    pallas_call x1, Pallas kernels, front(): pl.pallas_call(front_kernel, out_shape=(jax.ShapeDtypeStruct((quarter, 4...  6.53 us
    unnamed x32, local copies, waits for them, and re-layouts  4.61 us
  transfers between devices with their start and end apart: 13, of which 5 were waited for; matrix products, arithmetic and copies ran while one was open for 8% of the time, Pallas kernels for 5%

profile of v3, /device:TPU:2, one launch (start us, length us, event | category | flops | bytes accessed | tf_op | source)
XLA Modules:
  0.0 227.0 jit_solution(17452209364374348275)
XLA Ops:
  1.3 12.0 %all-to-all-start = ((s32[64,1,32]{2,1,0:T(1,128)}), s32[64,1,32]{2,1,0:T(1,128)S(1)}, u32[]{:S(2)}, u32[]{:S(2)}) async-start(s32[64,1,32]{2,1,0:T(1,128)} %broadcast_in_dim.27), calls=%async_computation | async-start | bytes 65536 | tf_op jit(solution)/shard_map/all_to_all | solution.py:378
  14.5 2.8 %spread.1 = bf16[128,32,768]{2,1,0:T(8,128)(2,1)} custom-call(s32[32]{0:T(128)} %compare_select_fusion.slot_ref, bf16[32,32,768]{2,1,0:T(8,128)(2,1)} %bitcast.17), custom_call_target="tpu_custom_call" | custom-call | tf_op jit(solution)/shard_map/spread/pallas_call | solution.py:40
  17.3 4.5 %all-to-all-done = s32[64,1,32]{2,1,0:T(1,128)S(1)} async-done(((s32[64,1,32]{2,1,0:T(1,128)}), s32[64,1,32]{2,1,0:T(1,128)S(1)}, u32[]{:S(2)}, u32[]{:S(2)}) %all-to-all-start) | async-done | bytes 8224 | tf_op jit(solution)/shard_map/all_to_all | solution.py:378
  22.5 6.8 %all-to-all-start.1 = ((bf16[64,2,32,768]{3,2,1,0:T(8,128)(2,1)}), bf16[64,2,32,768]{3,2,1,0:T(8,128)(2,1)}, u32[]{:S(2)}, u32[]{:S(2)}) async-start(bf16[64,2,32,768]{3,2,1,0:T(8,128)(2,1)} %bitcast.16), calls=%async_computation.1 | async-start | bytes 12582912 | tf_op jit(solution)/shard_map/all_to_all | solution.py:371
  30.4 1.6 collective-permute-start
  32.0 1.6 collective-permute-start.1
  38.9 2.1 fusion.1
  44.1 1.5 subtract_reduce_fusion
  52.6 32.7 %collective-permute-done.2.refs_4_.affine_ref = f32[2,768]{1,0:T(2,128)S(1)} collective-permute-done((f32[2,768]{1,0:T(2,128)}, f32[2,768]{1,0:T(2,128)S(1)}, u32[]{:S(2)}, u32[]{:S(2)}) %collective-permute-start.2) | collective-permute-done | bytes 6176 | tf_op jit(solution)/shard_map/ppermute | solution.py:346
  85.3 83.5 %all-to-all-done.1 = bf16[64,2,32,768]{3,2,1,0:T(8,128)(2,1)} async-done(((bf16[64,2,32,768]{3,2,1,0:T(8,128)(2,1)}), bf16[64,2,32,768]{3,2,1,0:T(8,128)(2,1)}, u32[]{:S(2)}, u32[]{:S(2)}) %all-to-all-start.1) | async-done | bytes 6291488 | tf_op jit(solution)/shard_map/all_to_all | solution.py:371
  168.8 3.7 %settle.1.rows_ref = bf16[1024,768]{1,0:T(8,128)(2,1)} custom-call(s32[32]{0:T(128)} %select_reduce_fusion.source_ref, bf16[128,32,768]{2,1,0:T(8,128)(2,1)} %bitcast.8.rows_ref, s32[3]{0:T(128)} %pad_add_fusion.refs_0_.meta_ref, f32[1]{0:T(128)} %bitcast.5.refs_1_.scale_ref, bf16[768,768]{1,0:T(8,128)(2,1)} %collective-permute-done.refs_2_.value_weight_ref, ...), custom_call_target="tpu_custom_call" | custom-call | tf_op jit(solution)/shard_map/settle/pallas_call | solution.py:85
  173.7 1.4 copy-done.1
  176.5 6.5 %front.1 = (f32[96,128]{1,0:T(8,128)S(1)}, bf16[96,128]{1,0:T(8,128)(2,1)S(1)}) custom-call(s32[32]{0:T(128)S(1)} %copy-done.7, s32[3]{0:T(128)S(1)} %copy-done.8, f32[1]{0:T(128)} %bitcast.5.refs_1_.scale_ref, bf16[1024,768]{1,0:T(8,128)(2,1)S(1)} %copy-done.1, f32[1,768]{1,0:T(1,128)S(1)} %copy-done.6, f32[1,768]{1,0:T(1,128)S(1)} %copy-done.5, ...), custom_call_target="tpu_custom_call" | custom-call | tf_op jit(solution)/shard_map/front/pallas_call | solution.py:193
  183.6 3.2 %collective-permute-start.3 = (bf16[96,128]{1,0:T(8,128)(2,1)S(1)}, bf16[96,128]{1,0:T(8,128)(2,1)S(1)}, u32[]{:S(2)}, u32[]{:S(2)}) collective-permute-start(bf16[96,128]{1,0:T(8,128)(2,1)S(1)} %get-tuple-element.8), channel_id=1, source_target_pairs={{0,1},{1,2},{2,3},{3,4},{4,5},{5,6},{6,7},{7,8},{8,9},{9,10},{10,1... | collective-permute-start | bytes 73736 | tf_op jit(solution)/shard_map/ppermute | solution.py:346
  186.8 4.5 %collective-permute-start.4 = (bf16[96,128]{1,0:T(8,128)(2,1)S(1)}, bf16[96,128]{1,0:T(8,128)(2,1)S(1)}, u32[]{:S(2)}, u32[]{:S(2)}) collective-permute-start(bf16[96,128]{1,0:T(8,128)(2,1)S(1)} %get-tuple-element.8), channel_id=1, source_target_pairs={{1,0},{2,1},{3,2},{4,3},{5,4},{6,5},{7,6},{8,7},{9,8},{10,9},{11,1... | collective-permute-start | bytes 73736 | tf_op jit(solution)/shard_map/ppermute | solution.py:346
  191.3 1.9 collective-permute-start.5
  193.2 6.0 %collective-permute-start.6 = (bf16[96,128]{1,0:T(8,128)(2,1)S(1)}, bf16[96,128]{1,0:T(8,128)(2,1)S(1)}, u32[]{:S(2)}, u32[]{:S(2)}) collective-permute-start(bf16[96,128]{1,0:T(8,128)(2,1)S(1)} %get-tuple-element.8), channel_id=1, source_target_pairs={{2,0},{3,1},{4,2},{5,3},{6,4},{7,5},{8,6},{9,7},{10,8},{11,9},{12,... | collective-permute-start | bytes 73736 | tf_op jit(solution)/shard_map/ppermute | solution.py:346
  199.3 1.9 collective-permute-start.7
  201.3 6.7 %collective-permute-start.8 = (bf16[96,128]{1,0:T(8,128)(2,1)S(1)}, bf16[96,128]{1,0:T(8,128)(2,1)S(1)}, u32[]{:S(2)}, u32[]{:S(2)}) collective-permute-start(bf16[96,128]{1,0:T(8,128)(2,1)S(1)} %get-tuple-element.8), channel_id=1, source_target_pairs={{3,0},{4,1},{5,2},{6,3},{7,4},{8,5},{9,6},{10,7},{11,8},{12,9},{13... | collective-permute-start | bytes 73736 | tf_op jit(solution)/shard_map/ppermute | solution.py:346
  208.0 1.4 collective-permute-done.8.refs_5_
  210.0 1.8 middle.1
  211.9 2.0 collective-permute-start.9
  213.9 3.3 %collective-permute-done.9.attention_ref = bf16[112,128]{1,0:T(8,128)(2,1)S(1)} collective-permute-done((bf16[112,128]{1,0:T(8,128)(2,1)}, bf16[112,128]{1,0:T(8,128)(2,1)S(1)}, u32[]{:S(2)}, u32[]{:S(2)}) %collective-permute-start.9) | collective-permute-done | bytes 28704 | tf_op jit(solution)/shard_map/ppermute | solution.py:346
  217.2 9.7 %back.1 = bf16[1024,768]{1,0:T(8,128)(2,1)} custom-call(bf16[112,128]{1,0:T(8,128)(2,1)S(1)} %collective-permute-done.9.attention_ref, bf16[1024,768]{1,0:T(8,128)(2,1)} %collective-permute-done.10.rows_ref, f32[2,768]{1,0:T(2,128)S(1)} %copy-done.4, bf16[768,768]{1,0:T(8,128)(2,1)} %collective-permute-done.refs_2_.value_weight_ref, ...), custom_call_target="tpu_custom_call" | custom-call | tf_op jit(solution)/shard_map/back/pallas_call | solution.py:323
  (57 shorter events, 21.0 us)
Async XLA Ops:
  1.3 20.6 %all-to-all-start = ((s32[64,1,32]{2,1,0:T(1,128)}), s32[64,1,32]{2,1,0:T(1,128)S(1)}, u32[]{:S(2)}, u32[]{:S(2)}) async-start(s32[64,1,32]{2,1,0:T(1,128)} %broadcast_in_dim.27), calls=%async_computation | async-start | bytes 65536 | tf_op jit(solution)/shard_map/all_to_all | solution.py:378
  22.5 6.8 %copy-start = (bf16[1,768,2304]{2,1,0:T(8,128)(2,1)S(1)}, bf16[1,768,2304]{2,1,0:T(8,128)(2,1)}, u32[]{:S(2)}) copy-start(bf16[1,768,2304]{2,1,0:T(8,128)(2,1)} %param.12) | copy-start | bytes 10616836
  22.5 146.3 %all-to-all-start.1 = ((bf16[64,2,32,768]{3,2,1,0:T(8,128)(2,1)}), bf16[64,2,32,768]{3,2,1,0:T(8,128)(2,1)}, u32[]{:S(2)}, u32[]{:S(2)}) async-start(bf16[64,2,32,768]{3,2,1,0:T(8,128)(2,1)} %bitcast.16), calls=%async_computation.1 | async-start | bytes 12582912 | tf_op jit(solution)/shard_map/all_to_all | solution.py:371
  29.3 4.3 %copy-start.5 = (f32[1,768]{1,0:T(1,128)S(1)}, f32[1,768]{1,0:T(1,128)}, u32[]{:S(2)}) copy-start(f32[1,768]{1,0:T(1,128)} %bias_ref.1) | copy-start | bytes 9220
  29.3 4.3 %copy-start.6 = (f32[1,768]{1,0:T(1,128)S(1)}, f32[1,768]{1,0:T(1,128)}, u32[]{:S(2)}) copy-start(f32[1,768]{1,0:T(1,128)} %gain_ref.1) | copy-start | bytes 9220
  30.4 54.9 %collective-permute-start = (bf16[768,768]{1,0:T(8,128)(2,1)}, bf16[768,768]{1,0:T(8,128)(2,1)}, u32[]{:S(2)}, u32[]{:S(2)}) collective-permute-start(bf16[768,768]{1,0:T(8,128)(2,1)} %slice_bitcast_fusion), channel_id=1, source_target_pairs={{0,64},{64,128},{128,192},{192,0},{1,65},{65,129},{129,193},{193,1... | collective-permute-start | bytes 3538952 | tf_op jit(solution)/shard_map/ppermute | solution.py:346
  32.0 53.4 %collective-permute-start.1 = (bf16[768,768]{1,0:T(8,128)(2,1)}, bf16[768,768]{1,0:T(8,128)(2,1)}, u32[]{:S(2)}, u32[]{:S(2)}) collective-permute-start(bf16[768,768]{1,0:T(8,128)(2,1)} %bitcast.10), channel_id=1, source_target_pairs={{0,64},{64,128},{128,192},{192,0},{1,65},{65,129},{129,193},{193,1... | collective-permute-start | bytes 3538952 | tf_op jit(solution)/shard_map/ppermute | solution.py:346
  34.2 51.2 %collective-permute-start.2 = (f32[2,768]{1,0:T(2,128)}, f32[2,768]{1,0:T(2,128)S(1)}, u32[]{:S(2)}, u32[]{:S(2)}) collective-permute-start(f32[2,768]{1,0:T(2,128)} %pad_maximum_fusion), channel_id=1, source_target_pairs={{0,64},{64,128},{128,192},{192,0},{1,65},{65,129},{129,193},{193,1... | collective-permute-start | bytes 18440 | tf_op jit(solution)/shard_map/ppermute | solution.py:346
  85.3 83.5 %copy-start.3 = (f32[2,768]{1,0:T(2,128)}, f32[2,768]{1,0:T(2,128)S(1)}, u32[]{:S(2)}) copy-start(f32[2,768]{1,0:T(2,128)S(1)} %collective-permute-done.2.refs_4_.affine_ref) | copy-start | bytes 18436
  172.5 44.7 %collective-permute-start.10 = (bf16[1024,768]{1,0:T(8,128)(2,1)}, bf16[1024,768]{1,0:T(8,128)(2,1)}, u32[]{:S(2)}, u32[]{:S(2)}) collective-permute-start(bf16[1024,768]{1,0:T(8,128)(2,1)} %settle.1.rows_ref), channel_id=1, source_target_pairs={{0,64},{64,128},{128,192},{192,0},{1,65},{65,129},{129,193},{193,1... | collective-permute-start | bytes 4718600 | tf_op jit(solution)/shard_map/ppermute | solution.py:346
  173.7 1.4 copy-start.1
  176.5 40.7 %copy-start.4 = (f32[2,768]{1,0:T(2,128)S(1)}, f32[2,768]{1,0:T(2,128)}, u32[]{:S(2)}) copy-start(f32[2,768]{1,0:T(2,128)} %copy-done.3) | copy-start | bytes 18436
  183.6 15.6 %collective-permute-start.3 = (bf16[96,128]{1,0:T(8,128)(2,1)S(1)}, bf16[96,128]{1,0:T(8,128)(2,1)S(1)}, u32[]{:S(2)}, u32[]{:S(2)}) collective-permute-start(bf16[96,128]{1,0:T(8,128)(2,1)S(1)} %get-tuple-element.8), channel_id=1, source_target_pairs={{0,1},{1,2},{2,3},{3,4},{4,5},{5,6},{6,7},{7,8},{8,9},{9,10},{10,1... | collective-permute-start | bytes 73736 | tf_op jit(solution)/shard_map/ppermute | solution.py:346
  186.8 14.4 %collective-permute-start.4 = (bf16[96,128]{1,0:T(8,128)(2,1)S(1)}, bf16[96,128]{1,0:T(8,128)(2,1)S(1)}, u32[]{:S(2)}, u32[]{:S(2)}) collective-permute-start(bf16[96,128]{1,0:T(8,128)(2,1)S(1)} %get-tuple-element.8), channel_id=1, source_target_pairs={{1,0},{2,1},{3,2},{4,3},{5,4},{6,5},{7,6},{8,7},{9,8},{10,9},{11,1... | collective-permute-start | bytes 73736 | tf_op jit(solution)/shard_map/ppermute | solution.py:346
  191.3 16.6 %collective-permute-start.5 = (bf16[96,128]{1,0:T(8,128)(2,1)S(1)}, bf16[96,128]{1,0:T(8,128)(2,1)S(1)}, u32[]{:S(2)}, u32[]{:S(2)}) collective-permute-start(bf16[96,128]{1,0:T(8,128)(2,1)S(1)} %get-tuple-element.8), channel_id=1, source_target_pairs={{0,2},{1,3},{2,4},{3,5},{4,6},{5,7},{6,8},{7,9},{8,10},{9,11},{10,... | collective-permute-start | bytes 73736 | tf_op jit(solution)/shard_map/ppermute | solution.py:346
  193.2 14.7 %collective-permute-start.6 = (bf16[96,128]{1,0:T(8,128)(2,1)S(1)}, bf16[96,128]{1,0:T(8,128)(2,1)S(1)}, u32[]{:S(2)}, u32[]{:S(2)}) collective-permute-start(bf16[96,128]{1,0:T(8,128)(2,1)S(1)} %get-tuple-element.8), channel_id=1, source_target_pairs={{2,0},{3,1},{4,2},{5,3},{6,4},{7,5},{8,6},{9,7},{10,8},{11,9},{12,... | collective-permute-start | bytes 73736 | tf_op jit(solution)/shard_map/ppermute | solution.py:346
  199.3 10.1 %copy-start.10 = (bf16[96,128]{1,0:T(8,128)(2,1)}, bf16[96,128]{1,0:T(8,128)(2,1)S(1)}, u32[]{:S(2)}) copy-start(bf16[96,128]{1,0:T(8,128)(2,1)S(1)} %collective-permute-done.3.refs_0_) | copy-start | bytes 73732
  199.3 8.7 %collective-permute-start.7 = (bf16[96,128]{1,0:T(8,128)(2,1)S(1)}, bf16[96,128]{1,0:T(8,128)(2,1)S(1)}, u32[]{:S(2)}, u32[]{:S(2)}) collective-permute-start(bf16[96,128]{1,0:T(8,128)(2,1)S(1)} %get-tuple-element.8), channel_id=1, source_target_pairs={{0,3},{1,4},{2,5},{3,6},{4,7},{5,8},{6,9},{7,10},{8,11},{9,12},{10... | collective-permute-start | bytes 73736 | tf_op jit(solution)/shard_map/ppermute | solution.py:346
  201.2 8.2 %copy-start.11 = (bf16[96,128]{1,0:T(8,128)(2,1)}, bf16[96,128]{1,0:T(8,128)(2,1)S(1)}, u32[]{:S(2)}) copy-start(bf16[96,128]{1,0:T(8,128)(2,1)S(1)} %collective-permute-done.4.refs_1_) | copy-start | bytes 73732
  201.3 8.2 %collective-permute-start.8 = (bf16[96,128]{1,0:T(8,128)(2,1)S(1)}, bf16[96,128]{1,0:T(8,128)(2,1)S(1)}, u32[]{:S(2)}, u32[]{:S(2)}) collective-permute-start(bf16[96,128]{1,0:T(8,128)(2,1)S(1)} %get-tuple-element.8), channel_id=1, source_target_pairs={{3,0},{4,1},{5,2},{6,3},{7,4},{8,5},{9,6},{10,7},{11,8},{12,9},{13... | collective-permute-start | bytes 73736 | tf_op jit(solution)/shard_map/ppermute | solution.py:346
  207.9 1.5 copy-start.12
  207.9 1.5 copy-start.13
  208.0 1.5 copy-start.14
  211.9 5.3 %collective-permute-start.9 = (bf16[112,128]{1,0:T(8,128)(2,1)}, bf16[112,128]{1,0:T(8,128)(2,1)S(1)}, u32[]{:S(2)}, u32[]{:S(2)}) collective-permute-start(bf16[112,128]{1,0:T(8,128)(2,1)} %middle.1), channel_id=1, source_target_pairs={{0,64},{64,128},{128,192},{192,0},{1,65},{65,129},{129,193},{193,1... | collective-permute-start | bytes 86024 | tf_op jit(solution)/shard_map/ppermute | solution.py:346
  (5 other events, 3.2 us)
